TPU v7x, 32 devices: a whole 2x2x4 slice. The times are simulated.
32 devices in a mesh: parts: 2 (over y), space: 4 (over z), tm: 2 (over x), chan: 2 (over core).
Axes of the slice: x: 2, y: 2, z: 4, core: 2. Of those that a mesh axis runs over, the one named last changes fastest.
Arguments:
- events: int32 [16, 128, 128], P(('parts', 'tm'), 'space'), parts along dimension 0, may hold values 0 or 1
- soft_info: bfloat16 [16, 128, 128], P(('parts', 'tm'), 'space'), parts along dimension 0, may hold values from -6 to 6
- embed: float32 [4, 64], replicated, may hold values from -6 to 6
- soft_gain: float32 [64], replicated, may hold values from -6 to 6
- conv_weights: bfloat16 [3, 64, 1728], replicated, may hold values from -0.21875 to 0.21875
- conv_bias: float32 [3, 64], replicated, may hold values from -1.75 to 1.75
- readout_weight: float32 [64], replicated, may hold values from -0.75 to 0.75
Outputs:
- logits: float32 [16, 128, 128], P(('parts', 'tm'), 'space'), parts along dimension 0
There are 2 independent parts, one for each index of `parts`. A program takes and returns all parts, laid end to end along the dimension named above; an argument that names none is the same for every part. Nothing has to cross between parts.
All inputs are finite; a program needn't handle non-finite values. No bound on the sum of `events` on one device may be relied on, other than what follows from the above.
Results may differ from a plain program's by a relative error of at most 0.024.
Values may be sent and summed in bfloat16 or wider, within the bound.
No kernel may reach another device: no remote copies, remote signals or barrier semaphores. Data moves between devices by JAX's collectives and lax.ppermute only.
A program may use at most 64 MiB of HBM per device.

v0:
```python
import functools

import jax
import jax.numpy as jnp
from jax import lax
from jax.experimental import pallas as pl
from jax.experimental.pallas import tpu as pltpu
from jax.sharding import PartitionSpec as P

HALO = 8
SUB = 16
EDGE = 4
CHUNK = 8
BF = jnp.bfloat16
F32 = jnp.float32


def prep_kernel(layers, ch, w_ref, embed_ref, gain_ref, bias_ref, read_ref, wout_ref, ws_ref, bout_ref, rw_ref, wt_ref):
    lanes = 4 * ch
    taps = 27
    zero_half = jnp.zeros((ch, ch), F32)
    zero_block = jnp.zeros((2 * ch, 2 * ch), BF)
    for layer in range(layers):
        wt_ref[...] = w_ref[layer].astype(F32).T
        for dx in range(3):
            sets = []
            for dr in range(3):
                g = [wt_ref[pl.ds(dr * 9 + dy * 3 + dx, ch, stride=taps), :] for dy in range(3)]
                outer = (g[0] + g[2]) * 0.5
                inner = g[1] * 0.5
                sets.append((g[0], outer + inner, outer - inner, g[2]))
            for i in range(4):
                own = jnp.concatenate(
                    [
                        jnp.concatenate([sets[1][i], sets[0][i]], 1),
                        jnp.concatenate([sets[2][i], sets[1][i]], 1),
                    ],
                    0,
                ).astype(BF)
                side = jnp.concatenate(
                    [
                        jnp.concatenate([zero_half, sets[2][i]], 1),
                        jnp.concatenate([sets[0][i], zero_half], 1),
                    ],
                    0,
                ).astype(BF)
                for b in range(2):
                    a = dx + b
                    wout_ref[layer, i, pl.ds(a * 2 * ch, 2 * ch), pl.ds(b * 2 * ch, 2 * ch)] = own
                    wout_ref[layer, i, pl.ds(lanes * 2 + a * 2 * ch, 2 * ch), pl.ds(b * 2 * ch, 2 * ch)] = side
        for i in range(4):
            for base in (0, lanes * 2):
                wout_ref[layer, i, pl.ds(base + 6 * ch, 2 * ch), pl.ds(0, 2 * ch)] = zero_block
                wout_ref[layer, i, pl.ds(base, 2 * ch), pl.ds(2 * ch, 2 * ch)] = zero_block
        bout_ref[pl.ds(layer, 1), :] = jnp.concatenate([bias_ref[pl.ds(layer, 1), :]] * 4, 1)
    table = jnp.concatenate([embed_ref[...], gain_ref[...], jnp.zeros((3, ch), F32)], 0)
    table = jnp.concatenate([table] * 4, 1)
    table = jnp.concatenate([table] * 4, 0)
    group = lax.broadcasted_iota(jnp.int32, table.shape, 0) // 8
    table = jnp.where(group == lax.broadcasted_iota(jnp.int32, table.shape, 1) // ch, table, 0.0)
    high = table.astype(BF).astype(F32)
    ws_ref[...] = jnp.concatenate([high, table - high], 0).astype(BF)
    read = jnp.concatenate([read_ref[...]] * 4, 1)
    high = read.astype(BF).astype(F32)
    row = lax.broadcasted_iota(jnp.int32, (8, lanes), 0)
    read = jnp.where(row < 4, jnp.broadcast_to(high, (8, lanes)), jnp.broadcast_to(read - high, (8, lanes)))
    rw_ref[...] = jnp.where(row % 4 == lax.broadcasted_iota(jnp.int32, (8, lanes), 1) // ch, read, 0.0).astype(BF)


def prepare(conv_weights, embed, soft_gain, conv_bias, readout_weight):
    layers, ch, depth = conv_weights.shape
    vmem = pl.BlockSpec(memory_space=pltpu.VMEM)
    return pl.pallas_call(
        functools.partial(prep_kernel, layers, ch),
        out_shape=(
            jax.ShapeDtypeStruct((layers, 4, 16 * ch, 4 * ch), BF),
            jax.ShapeDtypeStruct((64, 4 * ch), BF),
            jax.ShapeDtypeStruct((8, 4 * ch), F32),
            jax.ShapeDtypeStruct((8, 4 * ch), BF),
        ),
        in_specs=[vmem] * 5,
        out_specs=(vmem,) * 4,
        scratch_shapes=[pltpu.VMEM((depth, ch), F32)],
        compiler_params=pltpu.CompilerParams(vmem_limit_bytes=20 << 20),
        cost_estimate=pl.CostEstimate(flops=0, bytes_accessed=20_000_000, transcendentals=0),
        name="prepare",
    )(conv_weights, embed, soft_gain[None], conv_bias, readout_weight[None])


def main_kernel(
    cfg,
    ev_ref, soft_ref, up_ref, down_ref, next_ref, nup_ref, ndown_ref,
    w_ref, ws_ref, b_ref, rw_ref,
    out_ref,
    c_ref, e_ref, o_ref, d_ref, f_ref, t_ref, m_ref,
):
    layers, tile, strip, cols, n_space, n_tm, n_chan = cfg
    pairs = strip // 2
    rows = strip + 2 * HALO
    slabs = cols // SUB
    half = slabs // 2
    block = half * SUB
    chan = lax.axis_index("chan")
    first_pair = (lax.axis_index("space") * n_chan + chan) * pairs
    all_pairs = n_space * tile // 2
    has_next = jnp.where(lax.axis_index("tm") < n_tm - 1, 1.0, 0.0).astype(F32)

    def lay(slot, up, body, down):
        d_ref[slot, pl.ds(0, HALO), :] = up.astype(F32)
        d_ref[slot, pl.ds(HALO, tile), :] = body.astype(F32)
        d_ref[slot, pl.ds(HALO + tile, HALO), :] = down.astype(F32)

    for window, source in ((0, 0), (2, 2), (1, None)):
        for r in range(2):
            slot = (window * 2 + r) * 2
            if source is None:
                for kind in range(2):
                    lay(slot + kind, nup_ref[kind, r], next_ref[kind, r], ndown_ref[kind, r])
            else:
                lay(slot, up_ref[0, source + r], ev_ref[source + r], down_ref[0, source + r])
                lay(slot + 1, up_ref[1, source + r], soft_ref[source + r], down_ref[1, source + r])

    start = chan * strip
    if strip % 8 == 0:
        start = pl.multiple_of(start, 8)
    gathered = jnp.concatenate([d_ref[k, pl.ds(start, rows), :] for k in range(12)], 0).astype(BF)

    def column(lane):
        q = lane // SUB
        return (lane % SUB) * slabs + 2 * (q % half) + q // half

    perm = (
        lax.broadcasted_iota(jnp.int32, (cols, cols), 0)
        == column(lax.broadcasted_iota(jnp.int32, (cols, cols), 1))
    ).astype(F32).astype(BF)
    gathered = jnp.dot(gathered, perm, preferred_element_type=F32)

    row_id = lax.broadcasted_iota(jnp.int32, (rows, cols), 0) - HALO + first_pair * 2
    inside = (row_id >= 0) & (row_id < 2 * all_pairs)
    odd = (row_id + lax.broadcasted_iota(jnp.int32, (rows, cols), 1) // block) % 2
    for window in range(3):
        for r in range(2):
            slot = (window * 2 + r) * 2
            code = 2.0 * odd.astype(F32) + gathered[slot * rows : (slot + 1) * rows]
            signal = gathered[(slot + 1) * rows : (slot + 2) * rows]
            feats = [jnp.where(inside & (code == float(k)), 1.0, 0.0) for k in range(4)]
            feats.append(jnp.where(inside, signal, 0.0))
            feats += [jnp.zeros((rows, cols), F32)] * 3
            for k, feat in enumerate(feats):
                f_ref[window, pl.ds((r * 8 + k) * rows, rows), :] = feat

    sub_row = lax.broadcasted_iota(jnp.int32, (SUB, 2 * 64), 0)

    def keep(ref, window, pair, value):
        lanes = value.shape[1]
        mid = lanes // 2
        slot = pair + EDGE
        ref[window, slot, pl.ds(1, half)] = value.reshape(half, SUB, lanes).astype(BF)
        last = pltpu.roll(value[block - SUB :, mid:], 1, 0)
        ref[window, slot, 0, :, mid:] = jnp.where(sub_row == 0, 0.0, last).astype(BF)
        head = pltpu.roll(value[:SUB, :mid], SUB - 1, 0)
        ref[window, slot, half + 1, :, :mid] = jnp.where(sub_row == SUB - 1, 0.0, head).astype(BF)

    lanes = ws_ref.shape[1]
    mid = lanes // 2
    for window, reach in ((0, 3), (1, 3), (2, 2)):
        for p in range(-reach, pairs + reach):
            at = 2 * p + HALO
            feats = jnp.concatenate(
                [f_ref[window, pl.ds(at + k, 16, stride=rows), :] for k in range(2)], 0
            )
            feats = jnp.concatenate([feats, feats], 0).astype(BF)
            value = lax.dot_general(
                feats, ws_ref[...], (((0,), (0,)), ((), ())), preferred_element_type=F32
            )
            for k, ref in enumerate((e_ref, o_ref)):
                part = value[:, k * mid : (k + 1) * mid]
                keep(ref, window, p, jnp.concatenate([part[:block], part[block:]], 1))
        if window < 2:
            for ref, p in ((o_ref, -reach - 1), (e_ref, pairs + reach)):
                ref[window, p + EDGE] = jnp.zeros((half + 2, SUB, lanes), BF)

    pieces = (
        (slice(1, half + 1), slice(0, lanes)),
        (slice(0, 1), slice(mid, lanes)),
        (slice(half + 1, half + 2), slice(0, mid)),
    )

    def transform(window, reach):
        low, n = EDGE - reach, pairs + 2 * reach
        for slab, lane in pieces:
            even = e_ref[window, pl.ds(low, n), slab, :, lane]
            after = e_ref[window, pl.ds(low + 1, n), slab, :, lane]
            odd_ = o_ref[window, pl.ds(low, n), slab, :, lane]
            before = o_ref[window, pl.ds(low - 1, n), slab, :, lane]
            c_ref[0, window, pl.ds(low, n), slab, :, lane] = before - odd_
            c_ref[1, window, pl.ds(low, n), slab, :, lane] = even + odd_
            c_ref[2, window, pl.ds(low, n), slab, :, lane] = odd_ - even
            c_ref[3, window, pl.ds(low, n), slab, :, lane] = even - after

    def taps(i, window, low, n):
        view = lambda slab, lane: c_ref[i, window, pl.ds(low, n), slab, :, lane].reshape(n * block, -1)
        return [
            view(slice(0, half), slice(mid, lanes)),
            view(slice(1, half + 1), slice(0, lanes)),
            view(slice(2, half + 2), slice(0, mid)),
        ]

    def layer_step(layer, windows, reach, side, chunk):
        depth = lanes * 4 if side else lanes * 2
        bias = b_ref[pl.ds(layer, 1), :]
        total = pairs + 2 * reach
        for begin in range(0, total, chunk):
            n = min(chunk, total - begin)
            low = EDGE - reach + begin
            spare = begin // chunk % 2
            for i in range(4):
                lhs = []
                for window in windows:
                    parts = taps(i, window, low, n)
                    if side:
                        parts += taps(i, 1, low, n)
                    lhs.append(jnp.concatenate(parts, 1))
                lhs = jnp.concatenate(lhs, 0) if len(lhs) > 1 else lhs[0]
                size = lhs.shape[0]
                m_ref[spare, i, pl.ds(0, size)] = jnp.dot(
                    lhs, w_ref[layer, i, pl.ds(0, depth), :], preferred_element_type=F32
                )
            m = [m_ref[spare, i, pl.ds(0, size)] for i in range(4)]
            base = m[1] + bias
            even = jnp.maximum(base + (m[0] + m[2]), 0.0)
            odd_ = jnp.maximum(base - (m[2] + m[3]), 0.0)
            for k, window in enumerate(windows):
                for q in range(n):
                    p = begin + q - reach
                    at = (k * n + q) * block
                    ev, od = even[at : at + block], odd_[at : at + block]
                    if p < 0 or p >= pairs:
                        spot = first_pair + p
                        ok = jnp.where((spot >= 0) & (spot < all_pairs), 1.0, 0.0).astype(F32)
                        ev, od = ev * ok, od * ok
                    keep(e_ref, window, p, ev)
                    keep(o_ref, window, p, od)

    reach_of = lambda extent: (extent + 1) // 2
    for layer in range(layers):
        reach = reach_of(2 * layers - 1 - layer)
        for window in range(2):
            transform(window, reach)
        layer_step(layer, (0, 1), reach, False, CHUNK // 2)

    def logits(window, at):
        for k, ref in enumerate((e_ref, o_ref)):
            final = ref[window, pl.ds(EDGE, pairs), pl.ds(1, half)].reshape(pairs * block, lanes)
            value = lax.dot_general(
                rw_ref[...], final, (((1,), (1,)), ((), ())), preferred_element_type=F32
            )
            value = value[:4] + value[4:]
            value = jnp.concatenate([value, jnp.zeros_like(value)], 0)
            value = jnp.concatenate([value[:, p * block : (p + 1) * block] for p in range(pairs)], 0)
            high = value.astype(BF)
            rest = value - high.astype(F32)
            mid_part = rest.astype(BF)
            stacked = jnp.concatenate([high, mid_part, (rest - mid_part.astype(F32)).astype(BF)], 0)
            lane = lax.broadcasted_iota(jnp.int32, (block, 2 * cols), 1)
            spot = column(lax.broadcasted_iota(jnp.int32, (block, 2 * cols), 0) + (lane // cols) * block)
            back = (spot == lane % cols).astype(F32).astype(BF)
            value = jnp.dot(stacked, back, preferred_element_type=F32)
            n = pairs * 8
            value = value[:n] + value[n : 2 * n] + value[2 * n :]
            t_ref[0] = value[:, :cols]
            t_ref[1] = value[:, cols:]
            for r in range(2):
                line = t_ref[0, pl.ds(r, pairs, stride=8), :] + t_ref[1, pl.ds(2 + r, pairs, stride=8), :]
                out_ref[at + r, pl.ds(k, pairs, stride=2), :] = line

    logits(0, 0)

    reach = reach_of(layers)
    lane_id = lax.broadcasted_iota(jnp.int32, (SUB, lanes), 1)
    is_next = (lane_id % mid) < mid // 2
    for ref in (e_ref, o_ref):
        for slot in range(EDGE - reach, EDGE + pairs + reach):
            own = ref[0, slot].astype(F32)
            after = ref[1, slot].astype(F32) * has_next
            ref[1, slot] = jnp.where(is_next[None], after, own).astype(BF)
    reach = reach_of(layers - 1)
    transform(1, reach)
    for layer in range(layers):
        reach = reach_of(layers - 1 - layer)
        transform(2, reach)
        layer_step(layer, (2,), reach, True, CHUNK // 2)
    logits(2, 2)


def decode(cfg, arrays, weights):
    layers, tile, strip, cols = cfg[:4]
    rows = strip + 2 * HALO
    pairs = strip // 2
    lanes = weights[1].shape[1]
    slabs = cols // SUB // 2 + 2
    rounds = arrays[0].shape[0]
    vmem = pl.BlockSpec(memory_space=pltpu.VMEM)
    return pl.pallas_call(
        functools.partial(main_kernel, cfg),
        out_shape=jax.ShapeDtypeStruct((rounds, strip, cols), F32),
        in_specs=[vmem] * 11,
        out_specs=vmem,
        scratch_shapes=[
            pltpu.VMEM((4, 3, pairs + 2 * EDGE, slabs, SUB, lanes), BF),
            pltpu.VMEM((3, pairs + 2 * EDGE, slabs, SUB, lanes), BF),
            pltpu.VMEM((3, pairs + 2 * EDGE, slabs, SUB, lanes), BF),
            pltpu.VMEM((12, tile + 2 * HALO, cols), F32),
            pltpu.VMEM((3, 16 * rows, cols), F32),
            pltpu.VMEM((2, pairs * 8, cols), F32),
            pltpu.VMEM((2, 4, CHUNK * (slabs - 2) * SUB, lanes), F32),
        ],
        compiler_params=pltpu.CompilerParams(vmem_limit_bytes=40 << 20),
        name="decode",
    )(*arrays, *weights)


def per_device(sizes, events, soft_info, embed, soft_gain, conv_weights, conv_bias, readout_weight):
    n_space, n_tm, n_chan = sizes
    rounds, tile, cols = events.shape
    layers = conv_weights.shape[0]
    strip = tile // n_chan
    first = rounds // 2
    both = jnp.stack([events.astype(BF), soft_info])
    ahead = both[:, :first]
    shift_tm = [(t, t - 1) for t in range(1, n_tm)]
    if n_chan == 2 and strip >= HALO:
        chan = lax.axis_index("chan")
        edge = jnp.where(chan == 0, both[:, :, tile - HALO :], both[:, :, :HALO])
        own, diag = [], []
        for s in range(n_space):
            for c in range(n_chan):
                to = s + (1 if c == 0 else -1)
                if not 0 <= to < n_space:
                    continue
                own.append((s * n_chan + c, to * n_chan + c))
                for t in range(1, n_tm):
                    diag.append(((s * n_tm + t) * n_chan + c, (to * n_tm + t - 1) * n_chan + c))
        up = down = lax.ppermute(edge, ("space", "chan"), own)
        nup = ndown = lax.ppermute(edge[:, :first], ("space", "tm", "chan"), diag)
    else:
        low, high = both[:, :, :HALO], both[:, :, tile - HALO :]

        def pairs_of(step):
            return [(s, s + step) for s in range(n_space) if 0 <= s + step < n_space]

        def cross(step):
            return [(s * n_tm + t, to * n_tm + t - 1) for s, to in pairs_of(step) for t in range(1, n_tm)]

        up = lax.ppermute(high, "space", pairs_of(1))
        down = lax.ppermute(low, "space", pairs_of(-1))
        nup = lax.ppermute(high[:, :first], ("space", "tm"), cross(1))
        ndown = lax.ppermute(low[:, :first], ("space", "tm"), cross(-1))
    following = lax.ppermute(ahead, "tm", shift_tm)
    weights = prepare(conv_weights, embed, soft_gain, conv_bias, readout_weight)
    cfg = (layers, tile, strip, cols, n_space, n_tm, n_chan)
    mine = decode(cfg, (events, soft_info, up, down, following, nup, ndown), weights)
    parts = [mine]
    for step in range(1, n_chan):
        parts.append(lax.ppermute(mine, "chan", [(c, (c - step) % n_chan) for c in range(n_chan)]))
    chan = lax.axis_index("chan")
    ordered = [lax.select_n((c - chan) % n_chan, *parts) for c in range(n_chan)]
    return jnp.concatenate(ordered, 1)


def solution(mesh):
    split = P(("parts", "tm"), "space", None)
    sizes = tuple(mesh.shape[axis] for axis in ("space", "tm", "chan"))
    return jax.shard_map(
        functools.partial(per_device, sizes),
        mesh=mesh,
        in_specs=(split, split, P(), P(), P(), P(), P()),
        out_specs=split,
        check_vma=False,
    )
```

profile of v0, /device:TPU:7, one launch (start us, length us, event | category | flops | bytes accessed | tf_op | source)
XLA Modules:
  0.0 32.6 jit_solution(7875352610626078159)
XLA Ops:
  0.0 0.8 %convert_bitcast_fusion = bf16[1,4,32,128]{3,2,1,0:T(8,128)(2,1)S(1)} fusion(s32[4,32,128]{2,1,0:T(8,128)} %ev_ref.1), kind=kLoop, calls=%fused_computation.2 | loop fusion | flops 16384 | bytes 98304 | tf_op jit(solution)/shard_map/stack | solution.py:329
  0.8 0.7 %pad_maximum_fusion.1 = bf16[2,2,32,128]{3,2,1,0:T(8,128)(2,1)S(1)} fusion(bf16[1,4,32,128]{3,2,1,0:T(8,128)(2,1)} %bitcast.5, bf16[1,4,32,128]{3,2,1,0:T(8,128)(2,1)S(1)} %convert_bitcast_fusion), kind=kLoop, calls=%fused_computation.1 | loop fusion | flops 16384 | bytes 98304 | tf_op jit(solution)/shard_map/stack | solution.py:329
  1.6 2.1 %collective-permute-start.1 = (bf16[2,2,32,128]{3,2,1,0:T(8,128)(2,1)S(1)}, bf16[2,2,32,128]{3,2,1,0:T(8,128)(2,1)S(1)}, u32[]{:S(2)}, u32[]{:S(2)}) collective-permute-start(bf16[2,2,32,128]{3,2,1,0:T(8,128)(2,1)S(1)} %pad_maximum_fusion.1), channel_id=1, source_target_pairs={{2,0},{3,1},{6,4},{7,5},{10,8},{11,9},{14,12},{15,13},{18,16},{19,... | collective-permute-start | bytes 98312 | tf_op jit(solution)/shard_map/ppermute | solution.py:359
  3.7 0.7 %maximum_select_fusion = bf16[2,4,8,128]{3,2,1,0:T(8,128)(2,1)S(1)} fusion(bf16[1,4,32,128]{3,2,1,0:T(8,128)(2,1)} %bitcast.6, bf16[1,4,32,128]{3,2,1,0:T(8,128)(2,1)S(1)} %convert_bitcast_fusion, pred[]{:T(512)S(6)} %eq.6), kind=kLoop, calls=%fused_computation.3 | loop fusion | flops 73728 | bytes 81921 | tf_op jit(solution)/shard_map/jit(_where)/select_n | solution.py:334
  4.5 1.3 %collective-permute-start = (bf16[2,4,8,128]{3,2,1,0:T(8,128)(2,1)S(1)}, bf16[2,4,8,128]{3,2,1,0:T(8,128)(2,1)S(1)}, u32[]{:S(2)}, u32[]{:S(2)}) collective-permute-start(bf16[2,4,8,128]{3,2,1,0:T(8,128)(2,1)S(1)} %maximum_select_fusion), channel_id=1, source_target_pairs={{0,4},{4,8},{5,1},{8,12},{9,5},{13,9},{2,6},{6,10},{7,3},{10,14},{... | collective-permute-start | bytes 49160 | tf_op jit(solution)/shard_map/ppermute | solution.py:344
  5.8 0.7 %collective-permute-start.2 = (bf16[2,2,8,128]{3,2,1,0:T(8,128)(2,1)S(1)}, bf16[2,2,8,128]{3,2,1,0:T(8,128)(2,1)S(1)}, u32[]{:S(2)}, u32[]{:S(2)}) collective-permute-start(bf16[2,2,8,128]{3,2,1,0:T(8,128)(2,1)S(1)} %slice.16), channel_id=1, source_target_pairs={{2,4},{6,8},{7,1},{10,12},{11,5},{15,9},{18,20},{22,24},{23,17},{2... | collective-permute-start | bytes 24584 | tf_op jit(solution)/shard_map/ppermute | solution.py:345
  6.4 0.0 copy-start
  6.4 1.1 %copy-done = bf16[3,64,1728]{2,1,0:T(8,128)(2,1)S(1)} copy-done((bf16[3,64,1728]{2,1,0:T(8,128)(2,1)S(1)}, bf16[3,64,1728]{2,1,0:T(8,128)(2,1)}, u32[]{:S(2)}) %copy-start) | copy-done | bytes 663576
  7.5 0.0 copy-start.3
  7.5 0.7 %copy-done.3 = f32[4,64]{1,0:T(4,128)S(1)} copy-done((f32[4,64]{1,0:T(4,128)S(1)}, f32[4,64]{1,0:T(4,128)}, u32[]{:S(2)}) %copy-start.3) | copy-done | bytes 1048
  8.2 0.0 copy-start.4
  8.2 0.7 %copy-done.4 = f32[3,64]{1,0:T(4,128)S(1)} copy-done((f32[3,64]{1,0:T(4,128)S(1)}, f32[3,64]{1,0:T(4,128)}, u32[]{:S(2)}) %copy-start.4) | copy-done | bytes 792
  8.9 0.0 copy-start.5
  8.9 0.7 %copy-done.5 = f32[64]{0:T(128)S(1)} copy-done((f32[64]{0:T(128)S(1)}, f32[64]{0:T(128)}, u32[]{:S(2)}) %copy-start.5) | copy-done | bytes 280
  9.5 0.0 copy-start.6
  9.6 0.7 %copy-done.6 = f32[64]{0:T(128)S(1)} copy-done((f32[64]{0:T(128)S(1)}, f32[64]{0:T(128)}, u32[]{:S(2)}) %copy-start.6) | copy-done | bytes 280
  10.2 1.4 %prepare.1 = (bf16[3,4,1024,256]{3,2,1,0:T(8,128)(2,1)S(1)}, bf16[64,256]{1,0:T(8,128)(2,1)S(1)}, f32[8,256]{1,0:T(8,128)S(1)}, bf16[8,256]{1,0:T(8,128)(2,1)S(1)}) custom-call(bf16[3,64,1728]{2,1,0:T(8,128)(2,1)S(1)} %copy-done, f32[4,64]{1,0:T(4,128)S(1)} %copy-done.3, f32[1,64]{1,0:T(1,128)S(1)} %bitcast.7, f32[3,64]{1,0:T(4,128)S(1)} %copy-done.4, ...), custom_call_target="tpu_custom_call" | custom-call | bytes 20000000 | tf_op jit(solution)/shard_map/prepare/pallas_call | solution.py:73
  11.7 0.0 collective-permute-done.2.nup_ref.ndown_ref
  11.7 0.0 collective-permute-done.up_ref.down_ref
  11.7 0.0 collective-permute-done.1.next_ref
  11.7 0.0 copy-start.1
  11.7 0.7 %copy-done.1 = bf16[4,32,128]{2,1,0:T(8,128)(2,1)S(1)} copy-done((bf16[4,32,128]{2,1,0:T(8,128)(2,1)S(1)}, bf16[4,32,128]{2,1,0:T(8,128)(2,1)}, u32[]{:S(2)}) %copy-start.1) | copy-done | bytes 32792
  12.4 0.0 copy-start.2
  12.4 0.8 %copy-done.2 = s32[4,32,128]{2,1,0:T(8,128)S(1)} copy-done((s32[4,32,128]{2,1,0:T(8,128)S(1)}, s32[4,32,128]{2,1,0:T(8,128)}, u32[]{:S(2)}) %copy-start.2) | copy-done | bytes 65560
  13.3 13.0 %decode.1 = f32[4,16,128]{2,1,0:T(8,128)S(1)} custom-call(s32[4,32,128]{2,1,0:T(8,128)S(1)} %copy-done.2, bf16[4,32,128]{2,1,0:T(8,128)(2,1)S(1)} %copy-done.1, bf16[2,4,8,128]{3,2,1,0:T(8,128)(2,1)S(1)} %collective-permute-done.up_ref.down_ref, bf16[2,4,8,128]{3,2,1,0:T(8,128)(2,1)S(1)} %collective-permute-done.up_ref.down_ref, ...), custom_call_target="tpu_custom_call" | custom-call | tf_op jit(solution)/shard_map/decode/pallas_call | solution.py:304
  26.2 4.9 %collective-permute-start.3 = (f32[4,16,128]{2,1,0:T(8,128)S(1)}, f32[4,16,128]{2,1,0:T(8,128)S(1)}, u32[]{:S(2)}, u32[]{:S(2)}) collective-permute-start(f32[4,16,128]{2,1,0:T(8,128)S(1)} %decode.1), channel_id=1, source_target_pairs={{0,1},{1,0},{2,3},{3,2},{4,5},{5,4},{6,7},{7,6},{8,9},{9,8},{10,11... | collective-permute-start | bytes 98312 | tf_op jit(solution)/shard_map/ppermute | solution.py:365
  31.1 0.9 %collective-permute-done.3 = f32[4,16,128]{2,1,0:T(8,128)S(1)} collective-permute-done((f32[4,16,128]{2,1,0:T(8,128)S(1)}, f32[4,16,128]{2,1,0:T(8,128)S(1)}, u32[]{:S(2)}, u32[]{:S(2)}) %collective-permute-start.3) | collective-permute-done | bytes 32800 | tf_op jit(solution)/shard_map/ppermute | solution.py:365
  32.0 0.6 %pad_maximum_fusion = f32[4,32,128]{2,1,0:T(8,128)} fusion(f32[4,16,128]{2,1,0:T(8,128)S(1)} %get-tuple-element.14, f32[4,16,128]{2,1,0:T(8,128)S(1)} %get-tuple-element.13), kind=kLoop, calls=%fused_computation | loop fusion | flops 16384 | bytes 131072 | tf_op jit(solution)/shard_map/concatenate | solution.py:368
  (2 shorter events, 0.0 us)
Async XLA Ops:
  1.6 10.1 %collective-permute-start.1 = (bf16[2,2,32,128]{3,2,1,0:T(8,128)(2,1)S(1)}, bf16[2,2,32,128]{3,2,1,0:T(8,128)(2,1)S(1)}, u32[]{:S(2)}, u32[]{:S(2)}) collective-permute-start(bf16[2,2,32,128]{3,2,1,0:T(8,128)(2,1)S(1)} %pad_maximum_fusion.1), channel_id=1, source_target_pairs={{2,0},{3,1},{6,4},{7,5},{10,8},{11,9},{14,12},{15,13},{18,16},{19,... | collective-permute-start | bytes 98312 | tf_op jit(solution)/shard_map/ppermute | solution.py:359
  4.5 7.2 %collective-permute-start = (bf16[2,4,8,128]{3,2,1,0:T(8,128)(2,1)S(1)}, bf16[2,4,8,128]{3,2,1,0:T(8,128)(2,1)S(1)}, u32[]{:S(2)}, u32[]{:S(2)}) collective-permute-start(bf16[2,4,8,128]{3,2,1,0:T(8,128)(2,1)S(1)} %maximum_select_fusion), channel_id=1, source_target_pairs={{0,4},{4,8},{5,1},{8,12},{9,5},{13,9},{2,6},{6,10},{7,3},{10,14},{... | collective-permute-start | bytes 49160 | tf_op jit(solution)/shard_map/ppermute | solution.py:344
  5.8 5.9 %collective-permute-start.2 = (bf16[2,2,8,128]{3,2,1,0:T(8,128)(2,1)S(1)}, bf16[2,2,8,128]{3,2,1,0:T(8,128)(2,1)S(1)}, u32[]{:S(2)}, u32[]{:S(2)}) collective-permute-start(bf16[2,2,8,128]{3,2,1,0:T(8,128)(2,1)S(1)} %slice.16), channel_id=1, source_target_pairs={{2,4},{6,8},{7,1},{10,12},{11,5},{15,9},{18,20},{22,24},{23,17},{2... | collective-permute-start | bytes 24584 | tf_op jit(solution)/shard_map/ppermute | solution.py:345
  6.4 1.1 %copy-start = (bf16[3,64,1728]{2,1,0:T(8,128)(2,1)S(1)}, bf16[3,64,1728]{2,1,0:T(8,128)(2,1)}, u32[]{:S(2)}) copy-start(bf16[3,64,1728]{2,1,0:T(8,128)(2,1)} %w_ref.1) | copy-start | bytes 1990660
  7.5 0.7 %copy-start.3 = (f32[4,64]{1,0:T(4,128)S(1)}, f32[4,64]{1,0:T(4,128)}, u32[]{:S(2)}) copy-start(f32[4,64]{1,0:T(4,128)} %embed_ref.1) | copy-start | bytes 3076
  8.2 0.7 %copy-start.4 = (f32[3,64]{1,0:T(4,128)S(1)}, f32[3,64]{1,0:T(4,128)}, u32[]{:S(2)}) copy-start(f32[3,64]{1,0:T(4,128)} %bias_ref.1) | copy-start | bytes 2308
  8.9 0.7 %copy-start.5 = (f32[64]{0:T(128)S(1)}, f32[64]{0:T(128)}, u32[]{:S(2)}) copy-start(f32[64]{0:T(128)} %param.10) | copy-start | bytes 772
  9.5 0.7 %copy-start.6 = (f32[64]{0:T(128)S(1)}, f32[64]{0:T(128)}, u32[]{:S(2)}) copy-start(f32[64]{0:T(128)} %param.13) | copy-start | bytes 772
  11.7 0.8 %copy-start.1 = (bf16[4,32,128]{2,1,0:T(8,128)(2,1)S(1)}, bf16[4,32,128]{2,1,0:T(8,128)(2,1)}, u32[]{:S(2)}) copy-start(bf16[4,32,128]{2,1,0:T(8,128)(2,1)} %soft_ref.1) | copy-start | bytes 98308
  12.4 0.8 %copy-start.2 = (s32[4,32,128]{2,1,0:T(8,128)S(1)}, s32[4,32,128]{2,1,0:T(8,128)}, u32[]{:S(2)}) copy-start(s32[4,32,128]{2,1,0:T(8,128)} %ev_ref.1) | copy-start | bytes 196612
  26.2 5.7 %collective-permute-start.3 = (f32[4,16,128]{2,1,0:T(8,128)S(1)}, f32[4,16,128]{2,1,0:T(8,128)S(1)}, u32[]{:S(2)}, u32[]{:S(2)}) collective-permute-start(f32[4,16,128]{2,1,0:T(8,128)S(1)} %decode.1), channel_id=1, source_target_pairs={{0,1},{1,0},{2,3},{3,2},{4,5},{5,4},{6,7},{7,6},{8,9},{9,8},{10,11... | collective-permute-start | bytes 98312 | tf_op jit(solution)/shard_map/ppermute | solution.py:365
where the time goes:
time: 33.1 us; the launch traced here: 32.6 us
  Pallas kernels  14.4 us (44%)
  starting transfers between devices  8.96 us (27%)
  local copies, waits for them, and re-layouts  5.36 us (16%)
  other arithmetic  2.94 us (9%)
  waiting for transfers between devices  0.87 us (3%)
    pallas_call x1, Pallas kernels, decode(): pl.pallas_call(functools.partial(main_kernel, cfg), out_shape=jax.ShapeDt...  13 us
    unnamed x14, local copies, waits for them, and re-layouts  5.36 us
    ppermute x1, starting transfers between devices, per_device(): lax.ppermute(mine, 'chan', [(c, (c - step) % n_chan) for c in range(n_cha...  4.87 us
    ppermute x1, starting transfers between devices, per_device(): following = lax.ppermute(ahead, 'tm', shift_tm)  2.15 us
    another operation x2, other arithmetic, per_device(): both = jnp.stack([events.astype(BF), soft_info])  1.57 us
    pallas_call x1, Pallas kernels, prepare(): pl.pallas_call(functools.partial(prep_kernel, layers, ch), out_shape=(jax...  1.44 us
    ppermute x1, starting transfers between devices, per_device(): up = down = lax.ppermute(edge, ('space', 'chan'), own)  1.28 us
    ppermute x1, waiting for transfers between devices, per_device(): lax.ppermute(mine, 'chan', [(c, (c - step) % n_chan) for c in range(n_cha...  0.86 us
  transfers between devices with their start and end apart: 4, of which 1 were waited for; matrix products, arithmetic and copies ran while one was open for 2% of the time, Pallas kernels for 4%

commit v1 on v0

--- a/solution.py
+++ b/solution.py
@@ -13,6 +13,60 @@
 CHUNK = 8
 BF = jnp.bfloat16
 F32 = jnp.float32
+
+
+def pack_kernel(n_chan, *refs):
+    ev_hbm, soft_hbm = refs[:2]
+    small_in, small_out = refs[2:7], refs[11:16]
+    both_ref, ahead_ref, edge_ref, first_ref = refs[7:11]
+    ev_ref, soft_ref, sems = refs[16:]
+    copies = [
+        pltpu.make_async_copy(source, target, sems.at[k])
+        for k, (source, target) in enumerate(
+            zip((ev_hbm, soft_hbm) + small_in, (ev_ref, soft_ref) + small_out)
+        )
+    ]
+    for copy in copies:
+        copy.start()
+    copies[0].wait()
+    copies[1].wait()
+    rounds, tile, _ = ev_ref.shape
+    lower = lax.axis_index("chan") < n_chan - 1
+    for r in range(rounds):
+        for kind, value in enumerate((ev_ref[r].astype(F32), soft_ref[r].astype(F32))):
+            narrow = value.astype(BF)
+            both_ref[kind, r] = narrow
+            edge = jnp.where(lower, value[tile - HALO :], value[:HALO]).astype(BF)
+            edge_ref[kind, r] = edge
+            if r < rounds // 2:
+                ahead_ref[kind, r] = narrow
+                first_ref[kind, r] = edge
+    for copy in copies[2:]:
+        copy.wait()
+
+
+def pack(n_chan, events, soft_info, small):
+    rounds, tile, cols = events.shape
+    vmem = pl.BlockSpec(memory_space=pltpu.VMEM)
+    outs = [
+        jax.ShapeDtypeStruct((2, rounds, tile, cols), BF),
+        jax.ShapeDtypeStruct((2, rounds // 2, tile, cols), BF),
+        jax.ShapeDtypeStruct((2, rounds, HALO, cols), BF),
+        jax.ShapeDtypeStruct((2, rounds // 2, HALO, cols), BF),
+    ] + [jax.ShapeDtypeStruct(x.shape, x.dtype) for x in small]
+    return pl.pallas_call(
+        functools.partial(pack_kernel, n_chan),
+        out_shape=outs,
+        in_specs=[pl.BlockSpec(memory_space=pltpu.HBM)] * 7,
+        out_specs=[vmem] * len(outs),
+        scratch_shapes=[
+            pltpu.VMEM(events.shape, jnp.int32),
+            pltpu.VMEM(soft_info.shape, BF),
+            pltpu.SemaphoreType.DMA((7,)),
+        ],
+        compiler_params=pltpu.CompilerParams(vmem_limit_bytes=8 << 20),
+        name="pack",
+    )(*[pltpu.with_memory_space_constraint(x, pltpu.HBM) for x in (events, soft_info, *small)])
 
 
 def prep_kernel(layers, ch, w_ref, embed_ref, gain_ref, bias_ref, read_ref, wout_ref, ws_ref, bout_ref, rw_ref, wt_ref):
@@ -84,12 +138,12 @@
         compiler_params=pltpu.CompilerParams(vmem_limit_bytes=20 << 20),
         cost_estimate=pl.CostEstimate(flops=0, bytes_accessed=20_000_000, transcendentals=0),
         name="prepare",
-    )(conv_weights, embed, soft_gain[None], conv_bias, readout_weight[None])
+    )(conv_weights, embed, soft_gain, conv_bias, readout_weight)
 
 
 def main_kernel(
     cfg,
-    ev_ref, soft_ref, up_ref, down_ref, next_ref, nup_ref, ndown_ref,
+    both_ref, up_ref, down_ref, next_ref, nup_ref, ndown_ref,
     w_ref, ws_ref, b_ref, rw_ref,
     out_ref,
     c_ref, e_ref, o_ref, d_ref, f_ref, t_ref, m_ref,
@@ -103,7 +157,7 @@
     chan = lax.axis_index("chan")
     first_pair = (lax.axis_index("space") * n_chan + chan) * pairs
     all_pairs = n_space * tile // 2
-    has_next = jnp.where(lax.axis_index("tm") < n_tm - 1, 1.0, 0.0).astype(F32)
+    has_next = lax.axis_index("tm") < n_tm - 1
 
     def lay(slot, up, body, down):
         d_ref[slot, pl.ds(0, HALO), :] = up.astype(F32)
@@ -117,8 +171,9 @@
                 for kind in range(2):
                     lay(slot + kind, nup_ref[kind, r], next_ref[kind, r], ndown_ref[kind, r])
             else:
-                lay(slot, up_ref[0, source + r], ev_ref[source + r], down_ref[0, source + r])
-                lay(slot + 1, up_ref[1, source + r], soft_ref[source + r], down_ref[1, source + r])
+                for kind in range(2):
+                    at = (kind, source + r)
+                    lay(slot + kind, up_ref[at], both_ref[at], down_ref[at])
 
     start = chan * strip
     if strip % 8 == 0:
@@ -282,7 +337,7 @@
     for ref in (e_ref, o_ref):
         for slot in range(EDGE - reach, EDGE + pairs + reach):
             own = ref[0, slot].astype(F32)
-            after = ref[1, slot].astype(F32) * has_next
+            after = jnp.where(has_next, ref[1, slot].astype(F32), 0.0)
             ref[1, slot] = jnp.where(is_next[None], after, own).astype(BF)
     reach = reach_of(layers - 1)
     transform(1, reach)
@@ -299,12 +354,12 @@
     pairs = strip // 2
     lanes = weights[1].shape[1]
     slabs = cols // SUB // 2 + 2
-    rounds = arrays[0].shape[0]
+    rounds = arrays[0].shape[1]
     vmem = pl.BlockSpec(memory_space=pltpu.VMEM)
     return pl.pallas_call(
         functools.partial(main_kernel, cfg),
         out_shape=jax.ShapeDtypeStruct((rounds, strip, cols), F32),
-        in_specs=[vmem] * 11,
+        in_specs=[vmem] * 10,
         out_specs=vmem,
         scratch_shapes=[
             pltpu.VMEM((4, 3, pairs + 2 * EDGE, slabs, SUB, lanes), BF),
@@ -325,41 +380,43 @@
     rounds, tile, cols = events.shape
     layers = conv_weights.shape[0]
     strip = tile // n_chan
-    first = rounds // 2
-    both = jnp.stack([events.astype(BF), soft_info])
-    ahead = both[:, :first]
-    shift_tm = [(t, t - 1) for t in range(1, n_tm)]
+    packed = pack(
+        n_chan,
+        events,
+        soft_info,
+        (conv_weights, embed, soft_gain[None], conv_bias, readout_weight[None]),
+    )
+    both, ahead, edge, edge_first = packed[:4]
+    back = [(t, (t - 1) % n_tm) for t in range(n_tm)]
+    following = lax.ppermute(ahead, "tm", back)
     if n_chan == 2 and strip >= HALO:
-        chan = lax.axis_index("chan")
-        edge = jnp.where(chan == 0, both[:, :, tile - HALO :], both[:, :, :HALO])
         own, diag = [], []
         for s in range(n_space):
-            for c in range(n_chan):
-                to = s + (1 if c == 0 else -1)
-                if not 0 <= to < n_space:
-                    continue
-                own.append((s * n_chan + c, to * n_chan + c))
-                for t in range(1, n_tm):
-                    diag.append(((s * n_tm + t) * n_chan + c, (to * n_tm + t - 1) * n_chan + c))
+            for c in range(2):
+                to = s + 1 - 2 * c
+                spot = (to, c) if 0 <= to < n_space else (s, 1 - c)
+                own.append((s * 2 + c, spot[0] * 2 + spot[1]))
+                for t, u in back:
+                    diag.append(((s * n_tm + t) * 2 + c, (spot[0] * n_tm + u) * 2 + spot[1]))
         up = down = lax.ppermute(edge, ("space", "chan"), own)
-        nup = ndown = lax.ppermute(edge[:, :first], ("space", "tm", "chan"), diag)
+        nup = ndown = lax.ppermute(edge_first, ("space", "tm", "chan"), diag)
     else:
         low, high = both[:, :, :HALO], both[:, :, tile - HALO :]
-
-        def pairs_of(step):
-            return [(s, s + step) for s in range(n_space) if 0 <= s + step < n_space]
+        first = rounds // 2
+
+        def ring(step):
+            return [(s, (s + step) % n_space) for s in range(n_space)]
 
         def cross(step):
-            return [(s * n_tm + t, to * n_tm + t - 1) for s, to in pairs_of(step) for t in range(1, n_tm)]
-
-        up = lax.ppermute(high, "space", pairs_of(1))
-        down = lax.ppermute(low, "space", pairs_of(-1))
+            return [(s * n_tm + t, to * n_tm + u) for s, to in ring(step) for t, u in back]
+
+        up = lax.ppermute(high, "space", ring(1))
+        down = lax.ppermute(low, "space", ring(-1))
         nup = lax.ppermute(high[:, :first], ("space", "tm"), cross(1))
         ndown = lax.ppermute(low[:, :first], ("space", "tm"), cross(-1))
-    following = lax.ppermute(ahead, "tm", shift_tm)
-    weights = prepare(conv_weights, embed, soft_gain, conv_bias, readout_weight)
+    weights = prepare(*packed[4:])
     cfg = (layers, tile, strip, cols, n_space, n_tm, n_chan)
-    mine = decode(cfg, (events, soft_info, up, down, following, nup, ndown), weights)
+    mine = decode(cfg, (both, up, down, following, nup, ndown), weights)
     parts = [mine]
     for step in range(1, n_chan):
         parts.append(lax.ppermute(mine, "chan", [(c, (c - step) % n_chan) for c in range(n_chan)]))

time: 33.1 us -> 24.2 us (0.73)
  the two profiles are of different devices: /device:TPU:7 before, /device:TPU:0 now
where the time goes in v1:
time: 24.2 us; the launch traced here: 23.8 us
  Pallas kernels  15.6 us (64%)
  starting transfers between devices  6.23 us (26%)
  waiting for transfers between devices  1.25 us (5%)
  other arithmetic  0.64 us (3%)
    pallas_call x1, Pallas kernels, decode(): pl.pallas_call(functools.partial(main_kernel, cfg), out_shape=jax.ShapeDt...  12.9 us
    ppermute x1, starting transfers between devices, per_device(): following = lax.ppermute(ahead, 'tm', back)  3.03 us
    ppermute x1, starting transfers between devices, per_device(): up = down = lax.ppermute(edge, ('space', 'chan'), own)  1.58 us
    ppermute x1, starting transfers between devices, per_device(): nup = ndown = lax.ppermute(edge_first, ('space', 'tm', 'chan'), diag)  1.55 us
    pallas_call x1, Pallas kernels, prepare(): pl.pallas_call(functools.partial(prep_kernel, layers, ch), out_shape=(jax...  1.44 us
    pallas_call x1, Pallas kernels, pack(): pl.pallas_call(functools.partial(pack_kernel, n_chan), out_shape=outs, in...  1.22 us
    ppermute x1, waiting for transfers between devices, per_device(): lax.ppermute(mine, 'chan', [(c, (c - step) % n_chan) for c in range(n_cha...  1.17 us
    concatenate x1, other arithmetic, per_device(): return jnp.concatenate(ordered, 1)  0.64 us
  transfers between devices with their start and end apart: 4, of which 2 were waited for; matrix products, arithmetic and copies ran while one was open for 0% of the time, Pallas kernels for 6%

profile of v1, /device:TPU:0, one launch (start us, length us, event | category | flops | bytes accessed | tf_op | source)
XLA Modules:
  0.0 23.8 jit_solution(13857915697355171983)
XLA Ops:
  0.0 1.2 %pack.1 = (bf16[2,4,32,128]{3,2,1,0:T(8,128)(2,1)S(1)}, bf16[2,2,32,128]{3,2,1,0:T(8,128)(2,1)S(1)}, bf16[2,4,8,128]{3,2,1,0:T(8,128)(2,1)S(1)}, bf16[2,2,8,128]...) custom-call(s32[4,32,128]{2,1,0:T(8,128)} %refs_0_.1, ...), custom_call_target="tpu_custom_call" | custom-call | tf_op jit(solution)/shard_map/pack/pallas_call | solution.py:57
  1.2 3.0 %collective-permute-start.1 = (bf16[2,2,32,128]{3,2,1,0:T(8,128)(2,1)S(1)}, bf16[2,2,32,128]{3,2,1,0:T(8,128)(2,1)S(1)}, u32[]{:S(2)}, u32[]{:S(2)}) collective-permute-start(bf16[2,2,32,128]{3,2,1,0:T(8,128)(2,1)S(1)} %get-tuple-element.20), channel_id=1, source_target_pairs={{0,2},{2,0},{1,3},{3,1},{4,6},{6,4},{5,7},{7,5},{8,10},{10,8},{9,1... | collective-permute-start | bytes 98312 | tf_op jit(solution)/shard_map/ppermute | solution.py:391
  4.3 1.6 %collective-permute-start = (bf16[2,4,8,128]{3,2,1,0:T(8,128)(2,1)S(1)}, bf16[2,4,8,128]{3,2,1,0:T(8,128)(2,1)S(1)}, u32[]{:S(2)}, u32[]{:S(2)}) collective-permute-start(bf16[2,4,8,128]{3,2,1,0:T(8,128)(2,1)S(1)} %get-tuple-element.19), channel_id=1, source_target_pairs={{0,4},{1,0},{4,8},{5,1},{8,12},{9,5},{12,13},{13,9},{2,6},{3,2},{6... | collective-permute-start | bytes 49160 | tf_op jit(solution)/shard_map/ppermute | solution.py:401
  5.8 1.5 %collective-permute-start.2 = (bf16[2,2,8,128]{3,2,1,0:T(8,128)(2,1)S(1)}, bf16[2,2,8,128]{3,2,1,0:T(8,128)(2,1)S(1)}, u32[]{:S(2)}, u32[]{:S(2)}) collective-permute-start(bf16[2,2,8,128]{3,2,1,0:T(8,128)(2,1)S(1)} %get-tuple-element.21), channel_id=1, source_target_pairs={{0,6},{2,4},{1,2},{3,0},{4,10},{6,8},{5,3},{7,1},{8,14},{10,12},{9... | collective-permute-start | bytes 24584 | tf_op jit(solution)/shard_map/ppermute | solution.py:402
  7.4 1.4 %prepare.1 = (bf16[3,4,1024,256]{3,2,1,0:T(8,128)(2,1)S(1)}, bf16[64,256]{1,0:T(8,128)(2,1)S(1)}, f32[8,256]{1,0:T(8,128)S(1)}, bf16[8,256]{1,0:T(8,128)(2,1)S(1)}) custom-call(bf16[3,64,1728]{2,1,0:T(8,128)(2,1)S(1)} %get-tuple-element.22.w_ref, f32[4,64]{1,0:T(4,128)S(1)} %get-tuple-element.23.embed_ref, f32[1,64]{1,0:T(1,128)S(1)} %get-tuple-element.24.gain_ref, ...), custom_call_target="tpu_custom_call" | custom-call | bytes 20000000 | tf_op jit(solution)/shard_map/prepare/pallas_call | solution.py:127
  8.8 0.1 collective-permute-done.2.nup_ref.ndown_ref
  8.9 0.0 collective-permute-done.up_ref.down_ref
  8.9 0.0 collective-permute-done.1.next_ref
  8.9 12.9 %decode.1 = f32[4,16,128]{2,1,0:T(8,128)S(1)} custom-call(bf16[2,4,32,128]{3,2,1,0:T(8,128)(2,1)S(1)} %get-tuple-element.18.both_ref, bf16[2,4,8,128]{3,2,1,0:T(8,128)(2,1)S(1)} %collective-permute-done.up_ref.down_ref, bf16[2,4,8,128]{3,2,1,0:T(8,128)(2,1)S(1)} %collective-permute-done.up_ref.down_ref, ...), custom_call_target="tpu_custom_call" | custom-call | tf_op jit(solution)/shard_map/decode/pallas_call | solution.py:359
  21.8 0.1 collective-permute-start.3
  21.9 1.2 %collective-permute-done.3 = f32[4,16,128]{2,1,0:T(8,128)S(1)} collective-permute-done((f32[4,16,128]{2,1,0:T(8,128)S(1)}, f32[4,16,128]{2,1,0:T(8,128)S(1)}, u32[]{:S(2)}, u32[]{:S(2)}) %collective-permute-start.3) | collective-permute-done | bytes 32800 | tf_op jit(solution)/shard_map/ppermute | solution.py:422
  23.1 0.6 %pad_maximum_fusion = f32[4,32,128]{2,1,0:T(8,128)} fusion(f32[4,16,128]{2,1,0:T(8,128)S(1)} %get-tuple-element.32, f32[4,16,128]{2,1,0:T(8,128)S(1)} %get-tuple-element.31), kind=kLoop, calls=%fused_computation | loop fusion | flops 16384 | bytes 131072 | tf_op jit(solution)/shard_map/concatenate | solution.py:425
  (1 shorter events, 0.0 us)
Async XLA Ops:
  1.2 7.7 %collective-permute-start.1 = (bf16[2,2,32,128]{3,2,1,0:T(8,128)(2,1)S(1)}, bf16[2,2,32,128]{3,2,1,0:T(8,128)(2,1)S(1)}, u32[]{:S(2)}, u32[]{:S(2)}) collective-permute-start(bf16[2,2,32,128]{3,2,1,0:T(8,128)(2,1)S(1)} %get-tuple-element.20), channel_id=1, source_target_pairs={{0,2},{2,0},{1,3},{3,1},{4,6},{6,4},{5,7},{7,5},{8,10},{10,8},{9,1... | collective-permute-start | bytes 98312 | tf_op jit(solution)/shard_map/ppermute | solution.py:391
  4.3 4.7 %collective-permute-start = (bf16[2,4,8,128]{3,2,1,0:T(8,128)(2,1)S(1)}, bf16[2,4,8,128]{3,2,1,0:T(8,128)(2,1)S(1)}, u32[]{:S(2)}, u32[]{:S(2)}) collective-permute-start(bf16[2,4,8,128]{3,2,1,0:T(8,128)(2,1)S(1)} %get-tuple-element.19), channel_id=1, source_target_pairs={{0,4},{1,0},{4,8},{5,1},{8,12},{9,5},{12,13},{13,9},{2,6},{3,2},{6... | collective-permute-start | bytes 49160 | tf_op jit(solution)/shard_map/ppermute | solution.py:401
  5.8 3.1 %collective-permute-start.2 = (bf16[2,2,8,128]{3,2,1,0:T(8,128)(2,1)S(1)}, bf16[2,2,8,128]{3,2,1,0:T(8,128)(2,1)S(1)}, u32[]{:S(2)}, u32[]{:S(2)}) collective-permute-start(bf16[2,2,8,128]{3,2,1,0:T(8,128)(2,1)S(1)} %get-tuple-element.21), channel_id=1, source_target_pairs={{0,6},{2,4},{1,2},{3,0},{4,10},{6,8},{5,3},{7,1},{8,14},{10,12},{9... | collective-permute-start | bytes 24584 | tf_op jit(solution)/shard_map/ppermute | solution.py:402
  21.8 1.3 %collective-permute-start.3 = (f32[4,16,128]{2,1,0:T(8,128)S(1)}, f32[4,16,128]{2,1,0:T(8,128)S(1)}, u32[]{:S(2)}, u32[]{:S(2)}) collective-permute-start(f32[4,16,128]{2,1,0:T(8,128)S(1)} %decode.1), channel_id=1, source_target_pairs={{0,1},{1,0},{2,3},{3,2},{4,5},{5,4},{6,7},{7,6},{8,9},{9,8},{10,11... | collective-permute-start | bytes 98312 | tf_op jit(solution)/shard_map/ppermute | solution.py:422

commit v2 on v1

v2 whole, which is shorter than its diff:
```python
import functools

import jax
import jax.numpy as jnp
from jax import lax
from jax.experimental import pallas as pl
from jax.experimental.pallas import tpu as pltpu
from jax.sharding import PartitionSpec as P

HALO = 8
SUB = 16
EDGE = 4
CHUNK = 13
BF = jnp.bfloat16
F32 = jnp.float32


def pack_kernel(n_chan, *refs):
    ev_hbm, soft_hbm = refs[:2]
    small_in, small_out = refs[2:7], refs[9:14]
    both_ref, edge_ref = refs[7:9]
    ev_ref, soft_ref, sems = refs[14:]
    copies = [
        pltpu.make_async_copy(source, target, sems.at[k])
        for k, (source, target) in enumerate(
            zip((ev_hbm, soft_hbm) + small_in, (ev_ref, soft_ref) + small_out)
        )
    ]
    for copy in copies:
        copy.start()
    copies[0].wait()
    copies[1].wait()
    rounds, tile, _ = ev_ref.shape
    lower = lax.axis_index("chan") < n_chan - 1
    for r in range(rounds):
        for kind, value in enumerate((ev_ref[r].astype(F32), soft_ref[r].astype(F32))):
            both_ref[kind, r] = value.astype(BF)
            edge_ref[kind, r] = jnp.where(lower, value[tile - HALO :], value[:HALO]).astype(BF)
    for copy in copies[2:]:
        copy.wait()


def pack(n_chan, events, soft_info, small):
    rounds, tile, cols = events.shape
    vmem = pl.BlockSpec(memory_space=pltpu.VMEM)
    outs = [
        jax.ShapeDtypeStruct((2, rounds, tile, cols), BF),
        jax.ShapeDtypeStruct((2, rounds, HALO, cols), BF),
    ] + [jax.ShapeDtypeStruct(x.shape, x.dtype) for x in small]
    return pl.pallas_call(
        functools.partial(pack_kernel, n_chan),
        out_shape=outs,
        in_specs=[pl.BlockSpec(memory_space=pltpu.HBM)] * 7,
        out_specs=[vmem] * len(outs),
        scratch_shapes=[
            pltpu.VMEM(events.shape, jnp.int32),
            pltpu.VMEM(soft_info.shape, BF),
            pltpu.SemaphoreType.DMA((7,)),
        ],
        compiler_params=pltpu.CompilerParams(vmem_limit_bytes=8 << 20),
        name="pack",
    )(*[pltpu.with_memory_space_constraint(x, pltpu.HBM) for x in (events, soft_info, *small)])


def prep_kernel(layers, ch, w_ref, embed_ref, gain_ref, bias_ref, read_ref, wout_ref, ws_ref, bout_ref, rw_ref, wt_ref):
    lanes = 4 * ch
    taps = 27
    zero_half = jnp.zeros((ch, ch), F32)
    zero_block = jnp.zeros((2 * ch, 2 * ch), BF)
    for layer in range(layers):
        wt_ref[...] = w_ref[layer].astype(F32).T
        for dx in range(3):
            sets = []
            for dr in range(3):
                g = [wt_ref[pl.ds(dr * 9 + dy * 3 + dx, ch, stride=taps), :] for dy in range(3)]
                outer = (g[0] + g[2]) * 0.5
                inner = g[1] * 0.5
                sets.append((g[0], outer + inner, outer - inner, g[2]))
            for i in range(4):
                own = jnp.concatenate(
                    [
                        jnp.concatenate([sets[1][i], sets[0][i]], 1),
                        jnp.concatenate([sets[2][i], sets[1][i]], 1),
                    ],
                    0,
                ).astype(BF)
                side = jnp.concatenate(
                    [
                        jnp.concatenate([zero_half, sets[2][i]], 1),
                        jnp.concatenate([sets[0][i], zero_half], 1),
                    ],
                    0,
                ).astype(BF)
                for b in range(2):
                    a = dx + b
                    wout_ref[layer, i, pl.ds(a * 2 * ch, 2 * ch), pl.ds(b * 2 * ch, 2 * ch)] = own
                    wout_ref[layer, i, pl.ds(lanes * 2 + a * 2 * ch, 2 * ch), pl.ds(b * 2 * ch, 2 * ch)] = side
        for i in range(4):
            for base in (0, lanes * 2):
                wout_ref[layer, i, pl.ds(base + 6 * ch, 2 * ch), pl.ds(0, 2 * ch)] = zero_block
                wout_ref[layer, i, pl.ds(base, 2 * ch), pl.ds(2 * ch, 2 * ch)] = zero_block
        bout_ref[pl.ds(layer, 1), :] = jnp.concatenate([bias_ref[pl.ds(layer, 1), :]] * 4, 1)
    table = jnp.concatenate([embed_ref[...], gain_ref[...], jnp.zeros((3, ch), F32)], 0)
    table = jnp.concatenate([table] * 4, 1)
    table = jnp.concatenate([table] * 4, 0)
    group = lax.broadcasted_iota(jnp.int32, table.shape, 0) // 8
    table = jnp.where(group == lax.broadcasted_iota(jnp.int32, table.shape, 1) // ch, table, 0.0)
    high = table.astype(BF).astype(F32)
    ws_ref[...] = jnp.concatenate([high, table - high], 0).astype(BF)
    read = jnp.concatenate([read_ref[...]] * 4, 1)
    high = read.astype(BF).astype(F32)
    row = lax.broadcasted_iota(jnp.int32, (8, lanes), 0)
    read = jnp.where(row < 4, jnp.broadcast_to(high, (8, lanes)), jnp.broadcast_to(read - high, (8, lanes)))
    rw_ref[...] = jnp.where(row % 4 == lax.broadcasted_iota(jnp.int32, (8, lanes), 1) // ch, read, 0.0).astype(BF)


def prepare(conv_weights, embed, soft_gain, conv_bias, readout_weight):
    layers, ch, depth = conv_weights.shape
    vmem = pl.BlockSpec(memory_space=pltpu.VMEM)
    return pl.pallas_call(
        functools.partial(prep_kernel, layers, ch),
        out_shape=(
            jax.ShapeDtypeStruct((layers, 4, 16 * ch, 4 * ch), BF),
            jax.ShapeDtypeStruct((64, 4 * ch), BF),
            jax.ShapeDtypeStruct((8, 4 * ch), F32),
            jax.ShapeDtypeStruct((8, 4 * ch), BF),
        ),
        in_specs=[vmem] * 5,
        out_specs=(vmem,) * 4,
        scratch_shapes=[pltpu.VMEM((depth, ch), F32)],
        compiler_params=pltpu.CompilerParams(vmem_limit_bytes=20 << 20),
        cost_estimate=pl.CostEstimate(flops=0, bytes_accessed=20_000_000, transcendentals=0),
        name="prepare",
    )(conv_weights, embed, soft_gain, conv_bias, readout_weight)


def window_kernel(n_chan, both_ref, up_ref, down_ref, own_ref, send_ref, d_ref):
    _, rounds, tile, _ = both_ref.shape
    strip = tile // n_chan
    start = lax.axis_index("chan") * strip
    if strip % 8 == 0:
        start = pl.multiple_of(start, 8)
    for r in range(rounds):
        for kind in range(2):
            slot = r * 2 + kind
            d_ref[slot, pl.ds(0, HALO), :] = up_ref[kind, r].astype(F32)
            d_ref[slot, pl.ds(HALO, tile), :] = both_ref[kind, r].astype(F32)
            d_ref[slot, pl.ds(HALO + tile, HALO), :] = down_ref[kind, r].astype(F32)
            value = d_ref[slot, pl.ds(start, strip + 2 * HALO), :].astype(BF)
            own_ref[kind, r] = value
            if r < rounds // 2:
                send_ref[kind, r] = value


def cut_window(n_chan, both, up, down):
    kinds, rounds, tile, cols = both.shape
    rows = tile // n_chan + 2 * HALO
    vmem = pl.BlockSpec(memory_space=pltpu.VMEM)
    return pl.pallas_call(
        functools.partial(window_kernel, n_chan),
        out_shape=(
            jax.ShapeDtypeStruct((kinds, rounds, rows, cols), BF),
            jax.ShapeDtypeStruct((kinds, rounds // 2, rows, cols), BF),
        ),
        in_specs=[vmem] * 3,
        out_specs=(vmem,) * 2,
        scratch_shapes=[pltpu.VMEM((kinds * rounds, tile + 2 * HALO, cols), F32)],
        compiler_params=pltpu.CompilerParams(vmem_limit_bytes=8 << 20),
        name="window",
    )(both, up, down)


class Strip:
    def __init__(self, cfg, lanes):
        self.layers, tile, strip, self.cols, n_space, n_tm, n_chan = cfg
        self.strip, self.pairs = strip, strip // 2
        self.rows = strip + 2 * HALO
        self.slabs = self.cols // SUB
        self.half = self.slabs // 2
        self.block = self.half * SUB
        self.lanes, self.mid = lanes, lanes // 2
        self.first_row = (lax.axis_index("space") * n_chan + lax.axis_index("chan")) * strip
        self.all_rows = n_space * tile
        self.has_next = lax.axis_index("tm") < n_tm - 1
        self.sub_row = lax.broadcasted_iota(jnp.int32, (SUB, self.mid), 0)

    def column(self, lane):
        q = lane // SUB
        return (lane % SUB) * self.slabs + 2 * (q % self.half) + q // self.half

    def features(self, arrays, f_ref):
        cols, rows = self.cols, self.rows
        perm = (
            lax.broadcasted_iota(jnp.int32, (cols, cols), 0)
            == self.column(lax.broadcasted_iota(jnp.int32, (cols, cols), 1))
        ).astype(F32).astype(BF)
        gathered = jnp.dot(jnp.concatenate(arrays, 0), perm, preferred_element_type=F32)
        row_id = lax.broadcasted_iota(jnp.int32, (rows, cols), 0) - HALO + self.first_row
        inside = (row_id >= 0) & (row_id < self.all_rows)
        odd = (row_id + lax.broadcasted_iota(jnp.int32, (rows, cols), 1) // self.block) % 2
        base = 2.0 * odd.astype(F32)
        for slot in range(0, len(arrays), 2):
            code = base + gathered[slot * rows : (slot + 1) * rows]
            signal = gathered[(slot + 1) * rows : (slot + 2) * rows]
            feats = [jnp.where(inside & (code == float(k)), 1.0, 0.0) for k in range(4)]
            feats.append(jnp.where(inside, signal, 0.0))
            feats += [jnp.zeros((rows, cols), F32)] * 3
            for k, feat in enumerate(feats):
                f_ref[slot // 4, pl.ds((slot // 2 % 2 * 8 + k) * rows, rows), :] = feat

    def keep(self, ref, pair, value):
        half, block, mid = self.half, self.block, self.mid
        slot = pair + EDGE
        ref[slot, pl.ds(1, half)] = value.reshape(half, SUB, self.lanes).astype(BF)
        last = pltpu.roll(value[block - SUB :, mid:], 1, 0)
        ref[slot, 0, :, mid:] = jnp.where(self.sub_row == 0, 0.0, last).astype(BF)
        head = pltpu.roll(value[:SUB, :mid], SUB - 1, 0)
        ref[slot, half + 1, :, :mid] = jnp.where(self.sub_row == SUB - 1, 0.0, head).astype(BF)

    def begin(self, f_ref, ws_ref, e_ref, o_ref, reach):
        block, mid = self.block, self.mid
        for p in range(-reach, self.pairs + reach):
            at = 2 * p + HALO
            feats = jnp.concatenate(
                [f_ref[pl.ds(at + k, 16, stride=self.rows), :] for k in range(2)], 0
            )
            feats = jnp.concatenate([feats, feats], 0).astype(BF)
            value = lax.dot_general(
                feats, ws_ref[...], (((0,), (0,)), ((), ())), preferred_element_type=F32
            )
            for k, ref in enumerate((e_ref, o_ref)):
                part = value[:, k * mid : (k + 1) * mid]
                self.keep(ref, p, jnp.concatenate([part[:block], part[block:]], 1))

    def reach(self, extent):
        return EDGE - (extent + 1) // 2, self.pairs + extent, extent % 2

    def transform(self, e_ref, o_ref, c_ref, extent):
        half, lanes, mid = self.half, self.lanes, self.mid
        low, n, shift = self.reach(extent)
        for slab, lane in (
            (slice(1, half + 1), slice(0, lanes)),
            (slice(0, 1), slice(mid, lanes)),
            (slice(half + 1, half + 2), slice(0, mid)),
        ):
            view = lambda ref, step: ref[pl.ds(low + step, n), slab, :, lane]
            if shift:
                d = (view(e_ref, 0), view(o_ref, 0), view(e_ref, 1), view(o_ref, 1))
            else:
                d = (view(o_ref, -1), view(e_ref, 0), view(o_ref, 0), view(e_ref, 1))
            for i, value in enumerate((d[0] - d[2], d[1] + d[2], d[2] - d[1], d[1] - d[3])):
                c_ref[i, pl.ds(low, n), slab, :, lane] = value

    def taps(self, c_ref, i, low, n):
        half, lanes, mid = self.half, self.lanes, self.mid
        view = lambda slab, lane: c_ref[i, pl.ds(low, n), slab, :, lane].reshape(n * self.block, -1)
        return [
            view(slice(0, half), slice(mid, lanes)),
            view(slice(1, half + 1), slice(0, lanes)),
            view(slice(2, half + 2), slice(0, mid)),
        ]

    def layer(self, index, sources, e_ref, o_ref, m_ref, w_ref, b_ref, extent):
        depth = self.lanes * 2 * len(sources)
        bias = b_ref[pl.ds(index, 1), :]
        low, n_all, shift = self.reach(extent)
        count = -(-n_all // CHUNK)
        edges = [n_all * k // count for k in range(count + 1)]
        for spare, (begin, end) in enumerate(zip(edges, edges[1:])):
            n = end - begin
            spare %= 2
            size = n * self.block
            for i in range(4):
                lhs = sum([self.taps(c_ref, i, low + begin, n) for c_ref in sources], [])
                m_ref[spare, i, pl.ds(0, size)] = jnp.dot(
                    jnp.concatenate(lhs, 1),
                    w_ref[index, i, pl.ds(0, depth), :],
                    preferred_element_type=F32,
                )
            m = [m_ref[spare, i, pl.ds(0, size)] for i in range(4)]
            base = m[1] + bias
            upper = jnp.maximum(base + (m[0] + m[2]), 0.0)
            lower = jnp.maximum(base - (m[2] + m[3]), 0.0)
            for q in range(n):
                p = low - EDGE + begin + q
                for k, value in enumerate((upper, lower)):
                    y = 2 * p + shift + k
                    row = value[q * self.block : (q + 1) * self.block]
                    if y < 0 or y >= self.strip:
                        spot = self.first_row + y
                        row = row * jnp.where((spot >= 0) & (spot < self.all_rows), 1.0, 0.0).astype(F32)
                    self.keep(o_ref if y % 2 else e_ref, y // 2, row)

    def logits(self, e_ref, o_ref, rw_ref, t_ref, out_ref, at):
        pairs, block, cols = self.pairs, self.block, self.cols
        lane = lax.broadcasted_iota(jnp.int32, (block, 2 * cols), 1)
        spot = self.column(lax.broadcasted_iota(jnp.int32, (block, 2 * cols), 0) + (lane // cols) * block)
        back = (spot == lane % cols).astype(F32).astype(BF)
        for k, ref in enumerate((e_ref, o_ref)):
            final = ref[pl.ds(EDGE, pairs), pl.ds(1, self.half)].reshape(pairs * block, self.lanes)
            value = lax.dot_general(
                rw_ref[...], final, (((1,), (1,)), ((), ())), preferred_element_type=F32
            )
            value = value[:4] + value[4:]
            value = jnp.concatenate([value, jnp.zeros_like(value)], 0)
            value = jnp.concatenate([value[:, p * block : (p + 1) * block] for p in range(pairs)], 0)
            high = value.astype(BF)
            rest = value - high.astype(F32)
            next_part = rest.astype(BF)
            stacked = jnp.concatenate([high, next_part, (rest - next_part.astype(F32)).astype(BF)], 0)
            value = jnp.dot(stacked, back, preferred_element_type=F32)
            n = pairs * 8
            value = value[:n] + value[n : 2 * n] + value[2 * n :]
            t_ref[0] = value[:, :cols]
            t_ref[1] = value[:, cols:]
            for r in range(2):
                line = t_ref[0, pl.ds(r, pairs, stride=8), :] + t_ref[1, pl.ds(2 + r, pairs, stride=8), :]
                out_ref[at + r, pl.ds(k, pairs, stride=2), :] = line


def first_kernel(cfg, own_ref, w_ref, ws_ref, b_ref, e0_ref, o0_ref, e2_ref, o2_ref, c_ref, f_ref, m_ref):
    s = Strip(cfg, ws_ref.shape[1])
    s.features([own_ref[kind, r] for r in range(4) for kind in range(2)], f_ref)
    s.begin(f_ref.at[0], ws_ref, e0_ref, o0_ref, s.layers)
    for layer in range(s.layers):
        extent = 2 * s.layers - 1 - layer
        s.transform(e0_ref, o0_ref, c_ref, extent)
        s.layer(layer, (c_ref,), e0_ref, o0_ref, m_ref, w_ref, b_ref, extent)
    s.begin(f_ref.at[1], ws_ref, e2_ref, o2_ref, (s.layers + 1) // 2)


def second_kernel(
    cfg, next_ref, e0_ref, o0_ref, e2_ref, o2_ref, w_ref, ws_ref, b_ref, rw_ref, out_ref,
    e_ref, o_ref, eb_ref, ob_ref, c_ref, side_ref, f_ref, m_ref, t_ref,
):
    s = Strip(cfg, ws_ref.shape[1])
    s.features([next_ref[kind, r] for r in range(2) for kind in range(2)], f_ref)
    s.begin(f_ref.at[0], ws_ref, e_ref, o_ref, s.layers)
    for layer in range(s.layers):
        extent = 2 * s.layers - 1 - layer
        s.transform(e_ref, o_ref, c_ref, extent)
        s.layer(layer, (c_ref,), e_ref, o_ref, m_ref, w_ref, b_ref, extent)
    s.logits(e0_ref, o0_ref, rw_ref, t_ref, out_ref, 0)
    lane_id = lax.broadcasted_iota(jnp.int32, (SUB, s.lanes), 1)
    is_next = (lane_id % s.mid) < s.mid // 2
    reach = (s.layers + 1) // 2
    for source, ref in ((e0_ref, e_ref), (o0_ref, o_ref)):
        for slot in range(EDGE - reach, EDGE + s.pairs + reach):
            after = jnp.where(s.has_next, ref[slot].astype(F32), 0.0)
            ref[slot] = jnp.where(is_next[None], after, source[slot].astype(F32)).astype(BF)
    sources = (e2_ref, o2_ref)
    side = (e_ref, o_ref)
    for layer in range(s.layers):
        extent = s.layers - 1 - layer
        s.transform(*sources, c_ref, extent)
        s.transform(*side, side_ref, extent)
        sources = (eb_ref, ob_ref)
        s.layer(layer, (c_ref, side_ref), *sources, m_ref, w_ref, b_ref, extent)
    s.logits(*sources, rw_ref, t_ref, out_ref, 2)


def row_buffer(cfg, lanes):
    return (cfg[2] // 2 + 2 * EDGE, cfg[3] // SUB // 2 + 2, SUB, lanes)


def scratch(cfg, lanes, windows):
    rows = cfg[2] + 2 * HALO
    block = cfg[3] // 2
    return (
        pltpu.VMEM((windows, 16 * rows, cfg[3]), F32),
        pltpu.VMEM((2, 4, CHUNK * block, lanes), F32),
    )


def first_half(cfg, own, weights):
    lanes = weights[1].shape[1]
    buffer = row_buffer(cfg, lanes)
    vmem = pl.BlockSpec(memory_space=pltpu.VMEM)
    return pl.pallas_call(
        functools.partial(first_kernel, cfg),
        out_shape=(jax.ShapeDtypeStruct(buffer, BF),) * 4,
        in_specs=[vmem] * 4,
        out_specs=(vmem,) * 4,
        scratch_shapes=[pltpu.VMEM((4,) + buffer, BF), *scratch(cfg, lanes, 2)],
        compiler_params=pltpu.CompilerParams(vmem_limit_bytes=30 << 20),
        cost_estimate=pl.CostEstimate(flops=2_500_000_000, bytes_accessed=20_000_000, transcendentals=0),
        name="first",
    )(own, *weights[:3])


def second_half(cfg, following, held, weights):
    lanes = weights[1].shape[1]
    buffer = row_buffer(cfg, lanes)
    vmem = pl.BlockSpec(memory_space=pltpu.VMEM)
    return pl.pallas_call(
        functools.partial(second_kernel, cfg),
        out_shape=jax.ShapeDtypeStruct((4, cfg[2], cfg[3]), F32),
        in_specs=[vmem] * 9,
        out_specs=vmem,
        scratch_shapes=[pltpu.VMEM(buffer, BF)] * 4
        + [pltpu.VMEM((4,) + buffer, BF)] * 2
        + [*scratch(cfg, lanes, 1), pltpu.VMEM((2, cfg[2] // 2 * 8, cfg[3]), F32)],
        compiler_params=pltpu.CompilerParams(vmem_limit_bytes=40 << 20),
        name="second",
    )(following, *held, *weights)


def per_device(sizes, events, soft_info, embed, soft_gain, conv_weights, conv_bias, readout_weight):
    n_space, n_tm, n_chan = sizes
    rounds, tile, cols = events.shape
    layers = conv_weights.shape[0]
    strip = tile // n_chan
    packed = pack(
        n_chan,
        events,
        soft_info,
        (conv_weights, embed, soft_gain[None], conv_bias, readout_weight[None]),
    )
    both, edge = packed[:2]
    if n_chan == 2 and strip >= HALO:
        chain = []
        for s in range(n_space):
            for c in range(2):
                to = s + 1 - 2 * c
                spot = (to, c) if 0 <= to < n_space else (s, 1 - c)
                chain.append((s * 2 + c, spot[0] * 2 + spot[1]))
        up = down = lax.ppermute(edge, ("space", "chan"), chain)
    else:
        ring = lambda step: [(s, (s + step) % n_space) for s in range(n_space)]
        up = lax.ppermute(both[:, :, tile - HALO :], "space", ring(1))
        down = lax.ppermute(both[:, :, :HALO], "space", ring(-1))
    weights = prepare(*packed[2:])
    own, send = cut_window(n_chan, both, up, down)
    following = lax.ppermute(send, "tm", [(t, (t - 1) % n_tm) for t in range(n_tm)])
    cfg = (layers, tile, strip, cols, n_space, n_tm, n_chan)
    held = first_half(cfg, own, weights)
    mine = second_half(cfg, following, held, weights)
    parts = [mine]
    for step in range(1, n_chan):
        parts.append(lax.ppermute(mine, "chan", [(c, (c - step) % n_chan) for c in range(n_chan)]))
    chan = lax.axis_index("chan")
    ordered = [lax.select_n((c - chan) % n_chan, *parts) for c in range(n_chan)]
    return jnp.concatenate(ordered, 1)


def solution(mesh):
    split = P(("parts", "tm"), "space", None)
    sizes = tuple(mesh.shape[axis] for axis in ("space", "tm", "chan"))
    return jax.shard_map(
        functools.partial(per_device, sizes),
        mesh=mesh,
        in_specs=(split, split, P(), P(), P(), P(), P()),
        out_specs=split,
        check_vma=False,
    )
```

time: 24.2 us -> 23 us (0.950); the launches traced: 23.8 us -> 22.9 us
  starting transfers between devices: 6.23 us -> 4.7 us
  Pallas kernels: 15.6 us -> 16.3 us
    ppermute x3 -> x2, starting transfers between devices: 6.16 us -> 4.62 us  [the longest x1 3.07 us: per_device(): up = down = lax.ppermute(edge, ('space', 'chan'), chain)]
    pallas_call x1 -> x3, Pallas kernels: 12.9 us -> 13.6 us  [the longest x1 9.54 us: second_half(): pl.pallas_call(functools.partial(second_kernel, cfg), out_shape=jax.Shape...]
  transfers between devices with their start and end apart: 4 -> 3, of which waited for: 2 -> 1; matrix products, arithmetic and copies ran while one was open for 0% -> 0% of each run, Pallas kernels for 6% -> 24%
where the time goes in v2:
time: 23 us; the launch traced here: 22.9 us
  Pallas kernels  16.3 us (71%)
  starting transfers between devices  4.7 us (20%)
  waiting for transfers between devices  1.17 us (5%)
  other arithmetic  0.64 us (3%)
    pallas_call x1, Pallas kernels, second_half(): pl.pallas_call(functools.partial(second_kernel, cfg), out_shape=jax.Shape...  9.54 us
    pallas_call x1, Pallas kernels, first_half(): pl.pallas_call(functools.partial(first_kernel, cfg), out_shape=(jax.Shape...  4.07 us
    ppermute x1, starting transfers between devices, per_device(): up = down = lax.ppermute(edge, ('space', 'chan'), chain)  3.07 us
    ppermute x1, starting transfers between devices, per_device(): lax.ppermute(send, 'tm', [(t, (t - 1) % n_tm) for t in range(n_tm)])  1.56 us
    pallas_call x1, Pallas kernels, prepare(): pl.pallas_call(functools.partial(prep_kernel, layers, ch), out_shape=(jax...  1.44 us
    pallas_call x1, Pallas kernels, pack(): pl.pallas_call(functools.partial(pack_kernel, n_chan), out_shape=outs, in...  1.22 us
    ppermute x1, waiting for transfers between devices, per_device(): lax.ppermute(mine, 'chan', [(c, (c - step) % n_chan) for c in range(n_cha...  1.17 us
    concatenate x1, other arithmetic, per_device(): return jnp.concatenate(ordered, 1)  0.64 us
  transfers between devices with their start and end apart: 3, of which 1 were waited for; matrix products, arithmetic and copies ran while one was open for 0% of the time, Pallas kernels for 24%

profile of v2, /device:TPU:0, one launch (start us, length us, event | category | flops | bytes accessed | tf_op | source)
XLA Modules:
  0.0 22.9 jit_solution(9701608010797124384)
XLA Ops:
  0.0 1.2 %pack.1 = (bf16[2,4,32,128]{3,2,1,0:T(8,128)(2,1)S(1)}, bf16[2,4,8,128]{3,2,1,0:T(8,128)(2,1)S(1)}, bf16[3,64,1728]{2,1,0:T(8,128)(2,1)S(1)}, f32[4,64]{1,0:T(4,...) custom-call(s32[4,32,128]{2,1,0:T(8,128)} %refs_0_.1, bf16[4,32,128]{2,1,0:T(8,128)(2,1)} %refs_1_.1, ...), custom_call_target="tpu_custom_call" | custom-call | tf_op jit(solution)/shard_map/pack/pallas_call | solution.py:50
  1.2 3.1 %collective-permute-start = (bf16[2,4,8,128]{3,2,1,0:T(8,128)(2,1)S(1)}, bf16[2,4,8,128]{3,2,1,0:T(8,128)(2,1)S(1)}, u32[]{:S(2)}, u32[]{:S(2)}) collective-permute-start(bf16[2,4,8,128]{3,2,1,0:T(8,128)(2,1)S(1)} %get-tuple-element.23), channel_id=1, source_target_pairs={{0,4},{1,0},{4,8},{5,1},{8,12},{9,5},{12,13},{13,9},{2,6},{3,2},{6... | collective-permute-start | bytes 49160 | tf_op jit(solution)/shard_map/ppermute | solution.py:427
  4.3 1.4 %prepare.1 = (bf16[3,4,1024,256]{3,2,1,0:T(8,128)(2,1)S(1)}, bf16[64,256]{1,0:T(8,128)(2,1)S(1)}, f32[8,256]{1,0:T(8,128)S(1)}, bf16[8,256]{1,0:T(8,128)(2,1)S(1)}) custom-call(bf16[3,64,1728]{2,1,0:T(8,128)(2,1)S(1)} %get-tuple-element.26.w_ref, f32[4,64]{1,0:T(4,128)S(1)} %get-tuple-element.27.embed_ref, f32[1,64]{1,0:T(1,128)S(1)} %get-tuple-element.28.gain_ref, ...), custom_call_target="tpu_custom_call" | custom-call | bytes 20000000 | tf_op jit(solution)/shard_map/prepare/pallas_call | solution.py:120
  5.8 0.0 collective-permute-done.up_ref.down_ref
  5.8 1.6 %collective-permute-start.1 = (bf16[2,2,32,128]{3,2,1,0:T(8,128)(2,1)S(1)}, bf16[2,2,32,128]{3,2,1,0:T(8,128)(2,1)S(1)}, u32[]{:S(2)}, u32[]{:S(2)}) collective-permute-start(bf16[2,2,32,128]{3,2,1,0:T(8,128)(2,1)S(1)} %get-tuple-element.24), channel_id=1, source_target_pairs={{0,2},{2,0},{1,3},{3,1},{4,6},{6,4},{5,7},{7,5},{8,10},{10,8},{9,1... | collective-permute-start | bytes 98312 | tf_op jit(solution)/shard_map/ppermute | solution.py:434
  7.4 4.1 %first.1 = (bf16[16,6,16,256]{3,2,1,0:T(8,128)(2,1)S(1)}, bf16[16,6,16,256]{3,2,1,0:T(8,128)(2,1)S(1)}, bf16[16,6,16,256]{3,2,1,0:T(8,128)(2,1)S(1)}, bf16[16,6,16,256]{3,2,1,0:T(8,128)(2,1)S(1)}) custom-call(bf16[2,4,32,128]{3,2,1,0:T(8,128)(2,1)S(1)} %get-tuple-element.25.own_ref, bf16[3,4,1024,256]{3,2,1,0:T(8,128)(2,1)S(1)} %get-tuple-element.31.w_ref, ...), custom_call_target="tpu_custom_call" | custom-call | flops 2500000000 | bytes 20000000 | tf_op jit(solution)/shard_map/first/pallas_call | solution.py:379
  11.4 0.0 collective-permute-done.1.next_ref
  11.4 9.5 %second.1 = f32[4,16,128]{2,1,0:T(8,128)S(1)} custom-call(bf16[2,2,32,128]{3,2,1,0:T(8,128)(2,1)S(1)} %collective-permute-done.1.next_ref, bf16[16,6,16,256]{3,2,1,0:T(8,128)(2,1)S(1)} %get-tuple-element.34.e0_ref, bf16[16,6,16,256]{3,2,1,0:T(8,128)(2,1)S(1)} %get-tuple-element.35.o0_ref, bf16[16,6,16,256]{3,2,1,0:T(8,128)(2,1)S(1)} %get-tuple-element.36.e2_ref, ...), custom_call_target="tpu_custom_call" | custom-call | tf_op jit(solution)/shard_map/second/pallas_call | solution.py:395
  21.0 0.1 collective-permute-start.2
  21.1 1.2 %collective-permute-done.2 = f32[4,16,128]{2,1,0:T(8,128)S(1)} collective-permute-done((f32[4,16,128]{2,1,0:T(8,128)S(1)}, f32[4,16,128]{2,1,0:T(8,128)S(1)}, u32[]{:S(2)}, u32[]{:S(2)}) %collective-permute-start.2) | collective-permute-done | bytes 32800 | tf_op jit(solution)/shard_map/ppermute | solution.py:440
  22.3 0.6 %pad_maximum_fusion = f32[4,32,128]{2,1,0:T(8,128)} fusion(f32[4,16,128]{2,1,0:T(8,128)S(1)} %get-tuple-element.40, f32[4,16,128]{2,1,0:T(8,128)S(1)} %get-tuple-element.39), kind=kLoop, calls=%fused_computation | loop fusion | flops 16384 | bytes 131072 | tf_op jit(solution)/shard_map/concatenate | solution.py:443
  (2 shorter events, 0.0 us)
Async XLA Ops:
  1.2 4.5 %collective-permute-start = (bf16[2,4,8,128]{3,2,1,0:T(8,128)(2,1)S(1)}, bf16[2,4,8,128]{3,2,1,0:T(8,128)(2,1)S(1)}, u32[]{:S(2)}, u32[]{:S(2)}) collective-permute-start(bf16[2,4,8,128]{3,2,1,0:T(8,128)(2,1)S(1)} %get-tuple-element.23), channel_id=1, source_target_pairs={{0,4},{1,0},{4,8},{5,1},{8,12},{9,5},{12,13},{13,9},{2,6},{3,2},{6... | collective-permute-start | bytes 49160 | tf_op jit(solution)/shard_map/ppermute | solution.py:427
  5.8 5.6 %collective-permute-start.1 = (bf16[2,2,32,128]{3,2,1,0:T(8,128)(2,1)S(1)}, bf16[2,2,32,128]{3,2,1,0:T(8,128)(2,1)S(1)}, u32[]{:S(2)}, u32[]{:S(2)}) collective-permute-start(bf16[2,2,32,128]{3,2,1,0:T(8,128)(2,1)S(1)} %get-tuple-element.24), channel_id=1, source_target_pairs={{0,2},{2,0},{1,3},{3,1},{4,6},{6,4},{5,7},{7,5},{8,10},{10,8},{9,1... | collective-permute-start | bytes 98312 | tf_op jit(solution)/shard_map/ppermute | solution.py:434
  21.0 1.3 %collective-permute-start.2 = (f32[4,16,128]{2,1,0:T(8,128)S(1)}, f32[4,16,128]{2,1,0:T(8,128)S(1)}, u32[]{:S(2)}, u32[]{:S(2)}) collective-permute-start(f32[4,16,128]{2,1,0:T(8,128)S(1)} %second.1), channel_id=1, source_target_pairs={{0,1},{1,0},{2,3},{3,2},{4,5},{5,4},{6,7},{7,6},{8,9},{9,8},{10,11... | collective-permute-start | bytes 98312 | tf_op jit(solution)/shard_map/ppermute | solution.py:440

commit v3 on v2

--- a/solution.py
+++ b/solution.py
@@ -62,13 +62,39 @@
     )(*[pltpu.with_memory_space_constraint(x, pltpu.HBM) for x in (events, soft_info, *small)])
 
 
-def prep_kernel(layers, ch, w_ref, embed_ref, gain_ref, bias_ref, read_ref, wout_ref, ws_ref, bout_ref, rw_ref, wt_ref):
+def open_weights(ch, embed_ref, gain_ref, wc_ref, wt_ref):
+    table = jnp.concatenate([embed_ref[...], gain_ref[...], jnp.zeros((3, ch), F32)], 0)
+    high = table.astype(BF)
+    table = jnp.concatenate([high.astype(F32), table - high.astype(F32)], 0).astype(BF)
+    zero = jnp.zeros((8, 2 * ch), F32)
+    pieces = {}
+    for dy in range(3):
+        for dx in range(3):
+            made = []
+            for dr in range(3):
+                tap = wt_ref[pl.ds(dr * 9 + dy * 3 + dx, ch, stride=27), :].astype(BF)
+                value = jnp.dot(table, tap, preferred_element_type=F32)
+                made.append(value[:8] + value[8:])
+            for r in range(2):
+                pieces[dy, dx, r] = jnp.concatenate([made[r + 1], made[r]], 1)
+    for a in range(4):
+        for j in range(4):
+            rows = [
+                jnp.concatenate([pieces.get((j - yp, a - xp, r), zero) for yp in range(2) for xp in range(2)], 1)
+                for r in range(2)
+            ]
+            wc_ref[pl.ds((a * 4 + j) * 16, 16), :] = jnp.concatenate(rows, 0).astype(BF)
+
+
+def prep_kernel(layers, ch, w_ref, embed_ref, gain_ref, bias_ref, read_ref, wout_ref, wc_ref, bout_ref, rw_ref, wt_ref):
     lanes = 4 * ch
     taps = 27
     zero_half = jnp.zeros((ch, ch), F32)
     zero_block = jnp.zeros((2 * ch, 2 * ch), BF)
     for layer in range(layers):
         wt_ref[...] = w_ref[layer].astype(F32).T
+        if layer == 0:
+            open_weights(ch, embed_ref, gain_ref, wc_ref, wt_ref)
         for dx in range(3):
             sets = []
             for dr in range(3):
@@ -93,20 +119,14 @@
                 ).astype(BF)
                 for b in range(2):
                     a = dx + b
-                    wout_ref[layer, i, pl.ds(a * 2 * ch, 2 * ch), pl.ds(b * 2 * ch, 2 * ch)] = own
+                    if layer > 0:
+                        wout_ref[layer, i, pl.ds(a * 2 * ch, 2 * ch), pl.ds(b * 2 * ch, 2 * ch)] = own
                     wout_ref[layer, i, pl.ds(lanes * 2 + a * 2 * ch, 2 * ch), pl.ds(b * 2 * ch, 2 * ch)] = side
         for i in range(4):
-            for base in (0, lanes * 2):
+            for base in (0, lanes * 2)[layer == 0 :]:
                 wout_ref[layer, i, pl.ds(base + 6 * ch, 2 * ch), pl.ds(0, 2 * ch)] = zero_block
                 wout_ref[layer, i, pl.ds(base, 2 * ch), pl.ds(2 * ch, 2 * ch)] = zero_block
         bout_ref[pl.ds(layer, 1), :] = jnp.concatenate([bias_ref[pl.ds(layer, 1), :]] * 4, 1)
-    table = jnp.concatenate([embed_ref[...], gain_ref[...], jnp.zeros((3, ch), F32)], 0)
-    table = jnp.concatenate([table] * 4, 1)
-    table = jnp.concatenate([table] * 4, 0)
-    group = lax.broadcasted_iota(jnp.int32, table.shape, 0) // 8
-    table = jnp.where(group == lax.broadcasted_iota(jnp.int32, table.shape, 1) // ch, table, 0.0)
-    high = table.astype(BF).astype(F32)
-    ws_ref[...] = jnp.concatenate([high, table - high], 0).astype(BF)
     read = jnp.concatenate([read_ref[...]] * 4, 1)
     high = read.astype(BF).astype(F32)
     row = lax.broadcasted_iota(jnp.int32, (8, lanes), 0)
@@ -121,7 +141,7 @@
         functools.partial(prep_kernel, layers, ch),
         out_shape=(
             jax.ShapeDtypeStruct((layers, 4, 16 * ch, 4 * ch), BF),
-            jax.ShapeDtypeStruct((64, 4 * ch), BF),
+            jax.ShapeDtypeStruct((256, 8 * ch), BF),
             jax.ShapeDtypeStruct((8, 4 * ch), F32),
             jax.ShapeDtypeStruct((8, 4 * ch), BF),
         ),
@@ -189,24 +209,49 @@
         return (lane % SUB) * self.slabs + 2 * (q % self.half) + q // self.half
 
     def features(self, arrays, f_ref):
-        cols, rows = self.cols, self.rows
-        perm = (
-            lax.broadcasted_iota(jnp.int32, (cols, cols), 0)
-            == self.column(lax.broadcasted_iota(jnp.int32, (cols, cols), 1))
-        ).astype(F32).astype(BF)
-        gathered = jnp.dot(jnp.concatenate(arrays, 0), perm, preferred_element_type=F32)
-        row_id = lax.broadcasted_iota(jnp.int32, (rows, cols), 0) - HALO + self.first_row
-        inside = (row_id >= 0) & (row_id < self.all_rows)
-        odd = (row_id + lax.broadcasted_iota(jnp.int32, (rows, cols), 1) // self.block) % 2
-        base = 2.0 * odd.astype(F32)
-        for slot in range(0, len(arrays), 2):
-            code = base + gathered[slot * rows : (slot + 1) * rows]
-            signal = gathered[(slot + 1) * rows : (slot + 2) * rows]
-            feats = [jnp.where(inside & (code == float(k)), 1.0, 0.0) for k in range(4)]
-            feats.append(jnp.where(inside, signal, 0.0))
-            feats += [jnp.zeros((rows, cols), F32)] * 3
-            for k, feat in enumerate(feats):
-                f_ref[slot // 4, pl.ds((slot // 2 % 2 * 8 + k) * rows, rows), :] = feat
+        cols, rows, block = self.cols, self.rows, self.block
+        shape = (2 * cols, 4 * cols)
+        source = lax.broadcasted_iota(jnp.int32, shape, 0)
+        lane = lax.broadcasted_iota(jnp.int32, shape, 1)
+        inner = lane % block
+        wanted = (inner % SUB) * self.slabs + 2 * (inner // SUB) + lane // cols - 1
+        select = (source % cols == wanted) & (source // cols == lane // block % 2)
+        stacked = jnp.concatenate(arrays, 0)
+        wide = jnp.concatenate(arrays, 0).astype(F32)
+        later = pltpu.roll(wide, wide.shape[0] - 2, 0).astype(BF)
+        gathered = jnp.dot(
+            jnp.concatenate([stacked, later], 1), select.astype(F32).astype(BF), preferred_element_type=F32
+        )
+        lane = lax.broadcasted_iota(jnp.int32, (rows, cols), 1)
+        row_id = lax.broadcasted_iota(jnp.int32, (rows, cols), 0) - HALO + self.first_row + 2 * (lane // block)
+        inner = lane % block
+        column = (inner % SUB) * self.slabs + 2 * (inner // SUB)
+        blank = jnp.zeros((rows, cols), F32)
+        for a in range(4):
+            x = column + (a - 1)
+            inside = (row_id >= 0) & (row_id < self.all_rows) & (x >= 0) & (x < cols)
+            base = jnp.where(inside, 2.0 * ((row_id + a + 1) % 2).astype(F32), -8.0)
+            for slot in range(0, len(arrays), 2):
+                code = base + gathered[slot * rows : (slot + 1) * rows, a * cols : (a + 1) * cols]
+                signal = gathered[(slot + 1) * rows : (slot + 2) * rows, a * cols : (a + 1) * cols]
+                feats = [jnp.where(code == float(k), 1.0, 0.0) for k in range(4)]
+                feats += [jnp.where(inside, signal, 0.0), blank, blank, blank]
+                for k, feat in enumerate(feats):
+                    f_ref[slot // 4, a, pl.ds((slot // 2 % 2 * 8 + k) * rows, rows), :] = feat
+
+    def opening(self, f_ref, wc_ref, open_ref, extent):
+        low, n_all, shift = self.reach(extent)
+        for q in range(0, n_all, 2):
+            at = 2 * (low - EDGE + q) + shift - 1 + HALO
+            feats = [f_ref[a, pl.ds(at + j, 16, stride=self.rows), :] for a in range(4) for j in range(4)]
+            value = lax.dot_general(
+                jnp.concatenate(feats, 0).astype(BF),
+                wc_ref[...],
+                (((0,), (0,)), ((), ())),
+                preferred_element_type=F32,
+            )
+            for k in range(2):
+                open_ref[k, pl.ds(q * self.block, 2 * self.block), :] = value[:, k * self.lanes : (k + 1) * self.lanes]
 
     def keep(self, ref, pair, value):
         half, block, mid = self.half, self.block, self.mid
@@ -216,21 +261,6 @@
         ref[slot, 0, :, mid:] = jnp.where(self.sub_row == 0, 0.0, last).astype(BF)
         head = pltpu.roll(value[:SUB, :mid], SUB - 1, 0)
         ref[slot, half + 1, :, :mid] = jnp.where(self.sub_row == SUB - 1, 0.0, head).astype(BF)
-
-    def begin(self, f_ref, ws_ref, e_ref, o_ref, reach):
-        block, mid = self.block, self.mid
-        for p in range(-reach, self.pairs + reach):
-            at = 2 * p + HALO
-            feats = jnp.concatenate(
-                [f_ref[pl.ds(at + k, 16, stride=self.rows), :] for k in range(2)], 0
-            )
-            feats = jnp.concatenate([feats, feats], 0).astype(BF)
-            value = lax.dot_general(
-                feats, ws_ref[...], (((0,), (0,)), ((), ())), preferred_element_type=F32
-            )
-            for k, ref in enumerate((e_ref, o_ref)):
-                part = value[:, k * mid : (k + 1) * mid]
-                self.keep(ref, p, jnp.concatenate([part[:block], part[block:]], 1))
 
     def reach(self, extent):
         return EDGE - (extent + 1) // 2, self.pairs + extent, extent % 2
@@ -260,8 +290,7 @@
             view(slice(2, half + 2), slice(0, mid)),
         ]
 
-    def layer(self, index, sources, e_ref, o_ref, m_ref, w_ref, b_ref, extent):
-        depth = self.lanes * 2 * len(sources)
+    def layer(self, index, sources, e_ref, o_ref, m_ref, w_ref, b_ref, extent, open_ref=None):
         bias = b_ref[pl.ds(index, 1), :]
         low, n_all, shift = self.reach(extent)
         count = -(-n_all // CHUNK)
@@ -270,17 +299,24 @@
             n = end - begin
             spare %= 2
             size = n * self.block
-            for i in range(4):
-                lhs = sum([self.taps(c_ref, i, low + begin, n) for c_ref in sources], [])
-                m_ref[spare, i, pl.ds(0, size)] = jnp.dot(
-                    jnp.concatenate(lhs, 1),
-                    w_ref[index, i, pl.ds(0, depth), :],
-                    preferred_element_type=F32,
-                )
-            m = [m_ref[spare, i, pl.ds(0, size)] for i in range(4)]
-            base = m[1] + bias
-            upper = jnp.maximum(base + (m[0] + m[2]), 0.0)
-            lower = jnp.maximum(base - (m[2] + m[3]), 0.0)
+            upper = lower = bias
+            if open_ref is not None:
+                at = pl.ds(begin * self.block, size)
+                upper, lower = open_ref[0, at, :] + bias, open_ref[1, at, :] + bias
+            if sources:
+                first = sources[0][1]
+                depth = self.lanes * 2 * len(sources)
+                for i in range(4):
+                    lhs = sum([self.taps(c_ref, i, low + begin, n) for c_ref, _ in sources], [])
+                    m_ref[spare, i, pl.ds(0, size)] = jnp.dot(
+                        jnp.concatenate(lhs, 1),
+                        w_ref[index, i, pl.ds(first, depth), :],
+                        preferred_element_type=F32,
+                    )
+                m = [m_ref[spare, i, pl.ds(0, size)] for i in range(4)]
+                upper = upper + m[1] + (m[0] + m[2])
+                lower = lower + m[1] - (m[2] + m[3])
+            upper, lower = jnp.maximum(upper, 0.0), jnp.maximum(lower, 0.0)
             for q in range(n):
                 p = low - EDGE + begin + q
                 for k, value in enumerate((upper, lower)):
@@ -318,28 +354,30 @@
                 out_ref[at + r, pl.ds(k, pairs, stride=2), :] = line
 
 
-def first_kernel(cfg, own_ref, w_ref, ws_ref, b_ref, e0_ref, o0_ref, e2_ref, o2_ref, c_ref, f_ref, m_ref):
-    s = Strip(cfg, ws_ref.shape[1])
+def run_first_window(s, f_ref, wc_ref, e_ref, o_ref, c_ref, m_ref, open_ref, w_ref, b_ref):
+    extent = 2 * s.layers - 1
+    s.opening(f_ref, wc_ref, open_ref, extent)
+    s.layer(0, (), e_ref, o_ref, m_ref, w_ref, b_ref, extent, open_ref)
+    for layer in range(1, s.layers):
+        extent -= 1
+        s.transform(e_ref, o_ref, c_ref, extent)
+        s.layer(layer, ((c_ref, 0),), e_ref, o_ref, m_ref, w_ref, b_ref, extent)
+
+
+def first_kernel(cfg, own_ref, w_ref, wc_ref, b_ref, e0_ref, o0_ref, start_ref, c_ref, f_ref, m_ref, open_ref):
+    s = Strip(cfg, b_ref.shape[1])
     s.features([own_ref[kind, r] for r in range(4) for kind in range(2)], f_ref)
-    s.begin(f_ref.at[0], ws_ref, e0_ref, o0_ref, s.layers)
-    for layer in range(s.layers):
-        extent = 2 * s.layers - 1 - layer
-        s.transform(e0_ref, o0_ref, c_ref, extent)
-        s.layer(layer, (c_ref,), e0_ref, o0_ref, m_ref, w_ref, b_ref, extent)
-    s.begin(f_ref.at[1], ws_ref, e2_ref, o2_ref, (s.layers + 1) // 2)
+    run_first_window(s, f_ref.at[0], wc_ref, e0_ref, o0_ref, c_ref, m_ref, open_ref, w_ref, b_ref)
+    s.opening(f_ref.at[1], wc_ref, start_ref, s.layers - 1)
 
 
 def second_kernel(
-    cfg, next_ref, e0_ref, o0_ref, e2_ref, o2_ref, w_ref, ws_ref, b_ref, rw_ref, out_ref,
-    e_ref, o_ref, eb_ref, ob_ref, c_ref, side_ref, f_ref, m_ref, t_ref,
+    cfg, next_ref, e0_ref, o0_ref, start_ref, w_ref, wc_ref, b_ref, rw_ref, out_ref,
+    e_ref, o_ref, eb_ref, ob_ref, c_ref, side_ref, f_ref, m_ref, open_ref, t_ref,
 ):
-    s = Strip(cfg, ws_ref.shape[1])
+    s = Strip(cfg, b_ref.shape[1])
     s.features([next_ref[kind, r] for r in range(2) for kind in range(2)], f_ref)
-    s.begin(f_ref.at[0], ws_ref, e_ref, o_ref, s.layers)
-    for layer in range(s.layers):
-        extent = 2 * s.layers - 1 - layer
-        s.transform(e_ref, o_ref, c_ref, extent)
-        s.layer(layer, (c_ref,), e_ref, o_ref, m_ref, w_ref, b_ref, extent)
+    run_first_window(s, f_ref.at[0], wc_ref, e_ref, o_ref, c_ref, m_ref, open_ref, w_ref, b_ref)
     s.logits(e0_ref, o0_ref, rw_ref, t_ref, out_ref, 0)
     lane_id = lax.broadcasted_iota(jnp.int32, (SUB, s.lanes), 1)
     is_next = (lane_id % s.mid) < s.mid // 2
@@ -348,39 +386,51 @@
         for slot in range(EDGE - reach, EDGE + s.pairs + reach):
             after = jnp.where(s.has_next, ref[slot].astype(F32), 0.0)
             ref[slot] = jnp.where(is_next[None], after, source[slot].astype(F32)).astype(BF)
-    sources = (e2_ref, o2_ref)
-    side = (e_ref, o_ref)
+    final = (eb_ref, ob_ref)
     for layer in range(s.layers):
         extent = s.layers - 1 - layer
-        s.transform(*sources, c_ref, extent)
-        s.transform(*side, side_ref, extent)
-        sources = (eb_ref, ob_ref)
-        s.layer(layer, (c_ref, side_ref), *sources, m_ref, w_ref, b_ref, extent)
-    s.logits(*sources, rw_ref, t_ref, out_ref, 2)
+        s.transform(e_ref, o_ref, side_ref, extent)
+        if layer == 0:
+            sources = ((side_ref, 2 * s.lanes),)
+        else:
+            s.transform(*final, c_ref, extent)
+            sources = ((c_ref, 0), (side_ref, 2 * s.lanes))
+        s.layer(layer, sources, *final, m_ref, w_ref, b_ref, extent, None if layer else start_ref)
+    s.logits(*final, rw_ref, t_ref, out_ref, 2)
 
 
 def row_buffer(cfg, lanes):
     return (cfg[2] // 2 + 2 * EDGE, cfg[3] // SUB // 2 + 2, SUB, lanes)
+
+
+def open_buffer(cfg, lanes, extent):
+    pairs = cfg[2] // 2 + extent
+    return (2, (pairs + pairs % 2) * cfg[3] // 2, lanes)
 
 
 def scratch(cfg, lanes, windows):
     rows = cfg[2] + 2 * HALO
     block = cfg[3] // 2
     return (
-        pltpu.VMEM((windows, 16 * rows, cfg[3]), F32),
+        pltpu.VMEM((windows, 4, 16 * rows, cfg[3]), F32),
         pltpu.VMEM((2, 4, CHUNK * block, lanes), F32),
+        pltpu.VMEM(open_buffer(cfg, lanes, 2 * cfg[0] - 1), F32),
     )
 
 
 def first_half(cfg, own, weights):
-    lanes = weights[1].shape[1]
+    lanes = weights[2].shape[1]
     buffer = row_buffer(cfg, lanes)
     vmem = pl.BlockSpec(memory_space=pltpu.VMEM)
     return pl.pallas_call(
         functools.partial(first_kernel, cfg),
-        out_shape=(jax.ShapeDtypeStruct(buffer, BF),) * 4,
+        out_shape=(
+            jax.ShapeDtypeStruct(buffer, BF),
+            jax.ShapeDtypeStruct(buffer, BF),
+            jax.ShapeDtypeStruct(open_buffer(cfg, lanes, cfg[0] - 1), F32),
+        ),
         in_specs=[vmem] * 4,
-        out_specs=(vmem,) * 4,
+        out_specs=(vmem,) * 3,
         scratch_shapes=[pltpu.VMEM((4,) + buffer, BF), *scratch(cfg, lanes, 2)],
         compiler_params=pltpu.CompilerParams(vmem_limit_bytes=30 << 20),
         cost_estimate=pl.CostEstimate(flops=2_500_000_000, bytes_accessed=20_000_000, transcendentals=0),
@@ -389,13 +439,13 @@
 
 
 def second_half(cfg, following, held, weights):
-    lanes = weights[1].shape[1]
+    lanes = weights[2].shape[1]
     buffer = row_buffer(cfg, lanes)
     vmem = pl.BlockSpec(memory_space=pltpu.VMEM)
     return pl.pallas_call(
         functools.partial(second_kernel, cfg),
         out_shape=jax.ShapeDtypeStruct((4, cfg[2], cfg[3]), F32),
-        in_specs=[vmem] * 9,
+        in_specs=[vmem] * 8,
         out_specs=vmem,
         scratch_shapes=[pltpu.VMEM(buffer, BF)] * 4
         + [pltpu.VMEM((4,) + buffer, BF)] * 2

time: 23 us -> 21.5 us (0.935)
  Pallas kernels: 16.3 us -> 14.6 us
    pallas_call x1, Pallas kernels: 9.54 us -> 8.22 us  [second_half(): pl.pallas_call(functools.partial(second_kernel, cfg), out_shape=jax.Shape...]
    pallas_call x1, Pallas kernels: 4.07 us -> 3.84 us  [first_half(): pl.pallas_call(functools.partial(first_kernel, cfg), out_shape=(jax.Shape...]
  transfers between devices with their start and end apart: 3 -> 3, of which waited for: 1 -> 2; matrix products, arithmetic and copies ran while one was open for 0% -> 0% of each run, Pallas kernels for 24% -> 24%
where the time goes in v3:
time: 21.5 us; the launch traced here: 21.3 us
  Pallas kernels  14.6 us (68%)
  starting transfers between devices  4.7 us (22%)
  waiting for transfers between devices  1.27 us (6%)
  other arithmetic  0.64 us (3%)
    pallas_call x1, Pallas kernels, second_half(): pl.pallas_call(functools.partial(second_kernel, cfg), out_shape=jax.Shape...  8.22 us
    pallas_call x1, Pallas kernels, first_half(): pl.pallas_call(functools.partial(first_kernel, cfg), out_shape=(jax.Shape...  3.84 us
    ppermute x1, starting transfers between devices, per_device(): up = down = lax.ppermute(edge, ('space', 'chan'), chain)  3.07 us
    ppermute x1, starting transfers between devices, per_device(): lax.ppermute(send, 'tm', [(t, (t - 1) % n_tm) for t in range(n_tm)])  1.56 us
    pallas_call x1, Pallas kernels, prepare(): pl.pallas_call(functools.partial(prep_kernel, layers, ch), out_shape=(jax...  1.33 us
    pallas_call x1, Pallas kernels, pack(): pl.pallas_call(functools.partial(pack_kernel, n_chan), out_shape=outs, in...  1.22 us
    ppermute x1, waiting for transfers between devices, per_device(): lax.ppermute(mine, 'chan', [(c, (c - step) % n_chan) for c in range(n_cha...  1.17 us
    concatenate x1, other arithmetic, per_device(): return jnp.concatenate(ordered, 1)  0.64 us
  transfers between devices with their start and end apart: 3, of which 2 were waited for; matrix products, arithmetic and copies ran while one was open for 0% of the time, Pallas kernels for 24%

profile of v3, /device:TPU:0, one launch (start us, length us, event | category | flops | bytes accessed | tf_op | source)
XLA Modules:
  0.0 21.3 jit_solution(12489674688748988734)
XLA Ops:
  0.0 1.2 %pack.1 = (bf16[2,4,32,128]{3,2,1,0:T(8,128)(2,1)S(1)}, bf16[2,4,8,128]{3,2,1,0:T(8,128)(2,1)S(1)}, bf16[3,64,1728]{2,1,0:T(8,128)(2,1)S(1)}, f32[4,64]{1,0:T(4,...) custom-call(s32[4,32,128]{2,1,0:T(8,128)} %refs_0_.1, bf16[4,32,128]{2,1,0:T(8,128)(2,1)} %refs_1_.1, ...), custom_call_target="tpu_custom_call" | custom-call | tf_op jit(solution)/shard_map/pack/pallas_call | solution.py:50
  1.2 3.1 %collective-permute-start = (bf16[2,4,8,128]{3,2,1,0:T(8,128)(2,1)S(1)}, bf16[2,4,8,128]{3,2,1,0:T(8,128)(2,1)S(1)}, u32[]{:S(2)}, u32[]{:S(2)}) collective-permute-start(bf16[2,4,8,128]{3,2,1,0:T(8,128)(2,1)S(1)} %get-tuple-element.22), channel_id=1, source_target_pairs={{0,4},{1,0},{4,8},{5,1},{8,12},{9,5},{12,13},{13,9},{2,6},{3,2},{6... | collective-permute-start | bytes 49160 | tf_op jit(solution)/shard_map/ppermute | solution.py:477
  4.3 1.3 %prepare.1 = (bf16[3,4,1024,256]{3,2,1,0:T(8,128)(2,1)S(1)}, bf16[256,512]{1,0:T(8,128)(2,1)S(1)}, f32[8,256]{1,0:T(8,128)S(1)}, bf16[8,256]{1,0:T(8,128)(2,1)S(1)}) custom-call(bf16[3,64,1728]{2,1,0:T(8,128)(2,1)S(1)} %get-tuple-element.25.w_ref, f32[4,64]{1,0:T(4,128)S(1)} %get-tuple-element.26.embed_ref, f32[1,64]{1,0:T(1,128)S(1)} %get-tuple-element.27.gain_ref, ...), custom_call_target="tpu_custom_call" | custom-call | bytes 20000000 | tf_op jit(solution)/shard_map/prepare/pallas_call | solution.py:140
  5.6 0.1 collective-permute-done.up_ref.down_ref
  5.8 1.6 %collective-permute-start.1 = (bf16[2,2,32,128]{3,2,1,0:T(8,128)(2,1)S(1)}, bf16[2,2,32,128]{3,2,1,0:T(8,128)(2,1)S(1)}, u32[]{:S(2)}, u32[]{:S(2)}) collective-permute-start(bf16[2,2,32,128]{3,2,1,0:T(8,128)(2,1)S(1)} %get-tuple-element.23), channel_id=1, source_target_pairs={{0,2},{2,0},{1,3},{3,1},{4,6},{6,4},{5,7},{7,5},{8,10},{10,8},{9,1... | collective-permute-start | bytes 98312 | tf_op jit(solution)/shard_map/ppermute | solution.py:484
  7.3 3.8 %first.1 = (bf16[16,6,16,256]{3,2,1,0:T(8,128)(2,1)S(1)}, bf16[16,6,16,256]{3,2,1,0:T(8,128)(2,1)S(1)}, f32[2,640,256]{2,1,0:T(8,128)S(1)}) custom-call(bf16[2,4,32,128]{3,2,1,0:T(8,128)(2,1)S(1)} %get-tuple-element.24.own_ref, bf16[3,4,1024,256]{3,2,1,0:T(8,128)(2,1)S(1)} %get-tuple-element.30.w_ref, bf16[256,512]{1,0:T(8,128)(2,1)S(1)} %get-tuple-element.31.wc_ref, ...), custom_call_target="tpu_custom_call" | custom-call | flops 2500000000 | bytes 20000000 | tf_op jit(solution)/shard_map/first/pallas_call | solution.py:425
  11.2 0.0 collective-permute-done.1.next_ref
  11.2 8.2 %second.1 = f32[4,16,128]{2,1,0:T(8,128)S(1)} custom-call(bf16[2,2,32,128]{3,2,1,0:T(8,128)(2,1)S(1)} %collective-permute-done.1.next_ref, bf16[16,6,16,256]{3,2,1,0:T(8,128)(2,1)S(1)} %get-tuple-element.33.e0_ref, bf16[16,6,16,256]{3,2,1,0:T(8,128)(2,1)S(1)} %get-tuple-element.34.o0_ref, f32[2,640,256]{2,1,0:T(8,128)S(1)} %get-tuple-element.35.start_ref, ...), custom_call_target="tpu_custom_call" | custom-call | tf_op jit(solution)/shard_map/second/pallas_call | solution.py:445
  19.4 0.1 collective-permute-start.2
  19.5 1.2 %collective-permute-done.2 = f32[4,16,128]{2,1,0:T(8,128)S(1)} collective-permute-done((f32[4,16,128]{2,1,0:T(8,128)S(1)}, f32[4,16,128]{2,1,0:T(8,128)S(1)}, u32[]{:S(2)}, u32[]{:S(2)}) %collective-permute-start.2) | collective-permute-done | bytes 32800 | tf_op jit(solution)/shard_map/ppermute | solution.py:490
  20.7 0.6 %pad_maximum_fusion = f32[4,32,128]{2,1,0:T(8,128)} fusion(f32[4,16,128]{2,1,0:T(8,128)S(1)} %get-tuple-element.38, f32[4,16,128]{2,1,0:T(8,128)S(1)} %get-tuple-element.37), kind=kLoop, calls=%fused_computation | loop fusion | flops 16384 | bytes 131072 | tf_op jit(solution)/shard_map/concatenate | solution.py:493
  (2 shorter events, 0.0 us)
Async XLA Ops:
  1.2 4.5 %collective-permute-start = (bf16[2,4,8,128]{3,2,1,0:T(8,128)(2,1)S(1)}, bf16[2,4,8,128]{3,2,1,0:T(8,128)(2,1)S(1)}, u32[]{:S(2)}, u32[]{:S(2)}) collective-permute-start(bf16[2,4,8,128]{3,2,1,0:T(8,128)(2,1)S(1)} %get-tuple-element.22), channel_id=1, source_target_pairs={{0,4},{1,0},{4,8},{5,1},{8,12},{9,5},{12,13},{13,9},{2,6},{3,2},{6... | collective-permute-start | bytes 49160 | tf_op jit(solution)/shard_map/ppermute | solution.py:477
  5.8 5.4 %collective-permute-start.1 = (bf16[2,2,32,128]{3,2,1,0:T(8,128)(2,1)S(1)}, bf16[2,2,32,128]{3,2,1,0:T(8,128)(2,1)S(1)}, u32[]{:S(2)}, u32[]{:S(2)}) collective-permute-start(bf16[2,2,32,128]{3,2,1,0:T(8,128)(2,1)S(1)} %get-tuple-element.23), channel_id=1, source_target_pairs={{0,2},{2,0},{1,3},{3,1},{4,6},{6,4},{5,7},{7,5},{8,10},{10,8},{9,1... | collective-permute-start | bytes 98312 | tf_op jit(solution)/shard_map/ppermute | solution.py:484
  19.4 1.3 %collective-permute-start.2 = (f32[4,16,128]{2,1,0:T(8,128)S(1)}, f32[4,16,128]{2,1,0:T(8,128)S(1)}, u32[]{:S(2)}, u32[]{:S(2)}) collective-permute-start(f32[4,16,128]{2,1,0:T(8,128)S(1)} %second.1), channel_id=1, source_target_pairs={{0,1},{1,0},{2,3},{3,2},{4,5},{5,4},{6,7},{7,6},{8,9},{9,8},{10,11... | collective-permute-start | bytes 98312 | tf_op jit(solution)/shard_map/ppermute | solution.py:490

commit v4 on v3

--- a/solution.py
+++ b/solution.py
@@ -13,6 +13,14 @@
 CHUNK = 13
 BF = jnp.bfloat16
 F32 = jnp.float32
+
+
+def quotient(value, by):
+    return lax.shift_right_logical(value, by.bit_length() - 1) if by & (by - 1) == 0 else value // by
+
+
+def remainder(value, by):
+    return value & (by - 1) if by & (by - 1) == 0 else value % by
 
 
 def pack_kernel(n_chan, *refs):
@@ -77,13 +85,23 @@
                 made.append(value[:8] + value[8:])
             for r in range(2):
                 pieces[dy, dx, r] = jnp.concatenate([made[r + 1], made[r]], 1)
+    blocks = []
     for a in range(4):
         for j in range(4):
             rows = [
                 jnp.concatenate([pieces.get((j - yp, a - xp, r), zero) for yp in range(2) for xp in range(2)], 1)
                 for r in range(2)
             ]
-            wc_ref[pl.ds((a * 4 + j) * 16, 16), :] = jnp.concatenate(rows, 0).astype(BF)
+            blocks.append(jnp.concatenate(rows, 0))
+    shape = (wc_ref.shape[0], 256)
+    row = lax.broadcasted_iota(jnp.int32, shape, 0)
+    inner = remainder(row, 8)
+    group = quotient(row, 8)
+    a = (group >= 5).astype(jnp.int32) + (group >= 10).astype(jnp.int32) + (group >= 15).astype(jnp.int32)
+    old = (a * 8 + inner) * 8 + group - 5 * a
+    order = (old == lax.broadcasted_iota(jnp.int32, shape, 1)).astype(F32).astype(BF)
+    wide = jnp.concatenate(blocks, 0).astype(BF)
+    wc_ref[...] = jnp.dot(order, wide, preferred_element_type=F32).astype(BF)
 
 
 def prep_kernel(layers, ch, w_ref, embed_ref, gain_ref, bias_ref, read_ref, wout_ref, wc_ref, bout_ref, rw_ref, wt_ref):
@@ -131,7 +149,7 @@
     high = read.astype(BF).astype(F32)
     row = lax.broadcasted_iota(jnp.int32, (8, lanes), 0)
     read = jnp.where(row < 4, jnp.broadcast_to(high, (8, lanes)), jnp.broadcast_to(read - high, (8, lanes)))
-    rw_ref[...] = jnp.where(row % 4 == lax.broadcasted_iota(jnp.int32, (8, lanes), 1) // ch, read, 0.0).astype(BF)
+    rw_ref[...] = jnp.where(remainder(row, 4) == quotient(lax.broadcasted_iota(jnp.int32, (8, lanes), 1), ch), read, 0.0).astype(BF)
 
 
 def prepare(conv_weights, embed, soft_gain, conv_bias, readout_weight):
@@ -141,7 +159,7 @@
         functools.partial(prep_kernel, layers, ch),
         out_shape=(
             jax.ShapeDtypeStruct((layers, 4, 16 * ch, 4 * ch), BF),
-            jax.ShapeDtypeStruct((256, 8 * ch), BF),
+            jax.ShapeDtypeStruct((160, 8 * ch), BF),
             jax.ShapeDtypeStruct((8, 4 * ch), F32),
             jax.ShapeDtypeStruct((8, 4 * ch), BF),
         ),
@@ -205,45 +223,45 @@
         self.sub_row = lax.broadcasted_iota(jnp.int32, (SUB, self.mid), 0)
 
     def column(self, lane):
-        q = lane // SUB
-        return (lane % SUB) * self.slabs + 2 * (q % self.half) + q // self.half
+        q = quotient(lane, SUB)
+        return remainder(lane, SUB) * self.slabs + 2 * remainder(q, self.half) + quotient(q, self.half)
 
     def features(self, arrays, f_ref):
         cols, rows, block = self.cols, self.rows, self.block
         shape = (2 * cols, 4 * cols)
         source = lax.broadcasted_iota(jnp.int32, shape, 0)
-        lane = lax.broadcasted_iota(jnp.int32, shape, 1)
-        inner = lane % block
-        wanted = (inner % SUB) * self.slabs + 2 * (inner // SUB) + lane // cols - 1
-        select = (source % cols == wanted) & (source // cols == lane // block % 2)
+        lane = lax.broadcasted_iota(jnp.int32, (1, 4 * cols), 1)
+        inner = remainder(lane, block)
+        wanted = remainder(inner, SUB) * self.slabs + 2 * quotient(inner, SUB) + quotient(lane, cols) - 1
+        wanted = jnp.where((wanted >= 0) & (wanted < cols), wanted, -2 * cols)
+        wanted = wanted + cols * remainder(quotient(lane, block), 2)
+        select = (source == wanted).astype(F32).astype(BF)
         stacked = jnp.concatenate(arrays, 0)
-        wide = jnp.concatenate(arrays, 0).astype(F32)
+        wide = stacked.astype(F32)
         later = pltpu.roll(wide, wide.shape[0] - 2, 0).astype(BF)
-        gathered = jnp.dot(
-            jnp.concatenate([stacked, later], 1), select.astype(F32).astype(BF), preferred_element_type=F32
-        )
+        gathered = jnp.dot(jnp.concatenate([stacked, later], 1), select, preferred_element_type=F32)
         lane = lax.broadcasted_iota(jnp.int32, (rows, cols), 1)
-        row_id = lax.broadcasted_iota(jnp.int32, (rows, cols), 0) - HALO + self.first_row + 2 * (lane // block)
-        inner = lane % block
-        column = (inner % SUB) * self.slabs + 2 * (inner // SUB)
-        blank = jnp.zeros((rows, cols), F32)
+        row_id = lax.broadcasted_iota(jnp.int32, (rows, cols), 0) - HALO + self.first_row + 2 * quotient(lane, block)
+        inside_rows = (row_id >= 0) & (row_id < self.all_rows)
+        inner = remainder(lane, block)
+        column = remainder(inner, SUB) * self.slabs + 2 * quotient(inner, SUB)
         for a in range(4):
             x = column + (a - 1)
-            inside = (row_id >= 0) & (row_id < self.all_rows) & (x >= 0) & (x < cols)
-            base = jnp.where(inside, 2.0 * ((row_id + a + 1) % 2).astype(F32), -8.0)
+            inside = inside_rows & (x >= 0) & (x < cols)
+            base = jnp.where(inside, 2.0 * ((row_id + a + 1) & 1).astype(F32), -8.0)
+            keep = jnp.where(inside, 1.0, 0.0)
             for slot in range(0, len(arrays), 2):
                 code = base + gathered[slot * rows : (slot + 1) * rows, a * cols : (a + 1) * cols]
                 signal = gathered[(slot + 1) * rows : (slot + 2) * rows, a * cols : (a + 1) * cols]
-                feats = [jnp.where(code == float(k), 1.0, 0.0) for k in range(4)]
-                feats += [jnp.where(inside, signal, 0.0), blank, blank, blank]
+                feats = [jnp.where(code == float(k), 1.0, 0.0) for k in range(4)] + [signal * keep]
                 for k, feat in enumerate(feats):
-                    f_ref[slot // 4, a, pl.ds((slot // 2 % 2 * 8 + k) * rows, rows), :] = feat
+                    f_ref[slot // 4, a, k, pl.ds(slot // 2 % 2, rows, stride=2), :] = feat
 
     def opening(self, f_ref, wc_ref, open_ref, extent):
         low, n_all, shift = self.reach(extent)
         for q in range(0, n_all, 2):
             at = 2 * (low - EDGE + q) + shift - 1 + HALO
-            feats = [f_ref[a, pl.ds(at + j, 16, stride=self.rows), :] for a in range(4) for j in range(4)]
+            feats = [f_ref[a, k, pl.ds(2 * at, 8), :] for a in range(4) for k in range(5)]
             value = lax.dot_general(
                 jnp.concatenate(feats, 0).astype(BF),
                 wc_ref[...],
@@ -330,8 +348,8 @@
     def logits(self, e_ref, o_ref, rw_ref, t_ref, out_ref, at):
         pairs, block, cols = self.pairs, self.block, self.cols
         lane = lax.broadcasted_iota(jnp.int32, (block, 2 * cols), 1)
-        spot = self.column(lax.broadcasted_iota(jnp.int32, (block, 2 * cols), 0) + (lane // cols) * block)
-        back = (spot == lane % cols).astype(F32).astype(BF)
+        spot = self.column(lax.broadcasted_iota(jnp.int32, (block, 2 * cols), 0) + quotient(lane, cols) * block)
+        back = (spot == remainder(lane, cols)).astype(F32).astype(BF)
         for k, ref in enumerate((e_ref, o_ref)):
             final = ref[pl.ds(EDGE, pairs), pl.ds(1, self.half)].reshape(pairs * block, self.lanes)
             value = lax.dot_general(
@@ -341,12 +359,10 @@
             value = jnp.concatenate([value, jnp.zeros_like(value)], 0)
             value = jnp.concatenate([value[:, p * block : (p + 1) * block] for p in range(pairs)], 0)
             high = value.astype(BF)
-            rest = value - high.astype(F32)
-            next_part = rest.astype(BF)
-            stacked = jnp.concatenate([high, next_part, (rest - next_part.astype(F32)).astype(BF)], 0)
+            stacked = jnp.concatenate([high, (value - high.astype(F32)).astype(BF)], 0)
             value = jnp.dot(stacked, back, preferred_element_type=F32)
             n = pairs * 8
-            value = value[:n] + value[n : 2 * n] + value[2 * n :]
+            value = value[:n] + value[n:]
             t_ref[0] = value[:, :cols]
             t_ref[1] = value[:, cols:]
             for r in range(2):
@@ -380,12 +396,13 @@
     run_first_window(s, f_ref.at[0], wc_ref, e_ref, o_ref, c_ref, m_ref, open_ref, w_ref, b_ref)
     s.logits(e0_ref, o0_ref, rw_ref, t_ref, out_ref, 0)
     lane_id = lax.broadcasted_iota(jnp.int32, (SUB, s.lanes), 1)
-    is_next = (lane_id % s.mid) < s.mid // 2
+    is_next = remainder(lane_id, s.mid) < s.mid // 2
+    own_part = jnp.where(is_next, 0.0, 1.0).astype(BF)[None]
+    next_part = jnp.where(is_next & s.has_next, 1.0, 0.0).astype(BF)[None]
     reach = (s.layers + 1) // 2
     for source, ref in ((e0_ref, e_ref), (o0_ref, o_ref)):
         for slot in range(EDGE - reach, EDGE + s.pairs + reach):
-            after = jnp.where(s.has_next, ref[slot].astype(F32), 0.0)
-            ref[slot] = jnp.where(is_next[None], after, source[slot].astype(F32)).astype(BF)
+            ref[slot] = ref[slot] * next_part + source[slot] * own_part
     final = (eb_ref, ob_ref)
     for layer in range(s.layers):
         extent = s.layers - 1 - layer
@@ -412,7 +429,7 @@
     rows = cfg[2] + 2 * HALO
     block = cfg[3] // 2
     return (
-        pltpu.VMEM((windows, 4, 16 * rows, cfg[3]), F32),
+        pltpu.VMEM((windows, 4, 5, 2 * rows, cfg[3]), F32),
         pltpu.VMEM((2, 4, CHUNK * block, lanes), F32),
         pltpu.VMEM(open_buffer(cfg, lanes, 2 * cfg[0] - 1), F32),
     )

time: 21.5 us -> 19.9 us (0.926)
  Pallas kernels: 14.6 us -> 13.1 us
    pallas_call x1, Pallas kernels: 3.84 us -> 2.96 us  [first_half(): pl.pallas_call(functools.partial(first_kernel, cfg), out_shape=(jax.Shape...]
    pallas_call x1, Pallas kernels: 8.22 us -> 7.49 us  [second_half(): pl.pallas_call(functools.partial(second_kernel, cfg), out_shape=jax.Shape...]
  transfers between devices with their start and end apart: 3 -> 3, of which waited for: 2 -> 2; matrix products, arithmetic and copies ran while one was open for 0% -> 0% of each run, Pallas kernels for 24% -> 22%
where the time goes in v4:
time: 19.9 us; the launch traced here: 19.7 us
  Pallas kernels  13.1 us (66%)
  starting transfers between devices  4.69 us (24%)
  waiting for transfers between devices  1.26 us (6%)
  other arithmetic  0.64 us (3%)
    pallas_call x1, Pallas kernels, second_half(): pl.pallas_call(functools.partial(second_kernel, cfg), out_shape=jax.Shape...  7.49 us
    ppermute x1, starting transfers between devices, per_device(): up = down = lax.ppermute(edge, ('space', 'chan'), chain)  3.07 us
    pallas_call x1, Pallas kernels, first_half(): pl.pallas_call(functools.partial(first_kernel, cfg), out_shape=(jax.Shape...  2.96 us
    ppermute x1, starting transfers between devices, per_device(): lax.ppermute(send, 'tm', [(t, (t - 1) % n_tm) for t in range(n_tm)])  1.56 us
    pallas_call x1, Pallas kernels, prepare(): pl.pallas_call(functools.partial(prep_kernel, layers, ch), out_shape=(jax...  1.35 us
    pallas_call x1, Pallas kernels, pack(): pl.pallas_call(functools.partial(pack_kernel, n_chan), out_shape=outs, in...  1.22 us
    ppermute x1, waiting for transfers between devices, per_device(): lax.ppermute(mine, 'chan', [(c, (c - step) % n_chan) for c in range(n_cha...  1.17 us
    concatenate x1, other arithmetic, per_device(): return jnp.concatenate(ordered, 1)  0.64 us
  transfers between devices with their start and end apart: 3, of which 2 were waited for; matrix products, arithmetic and copies ran while one was open for 0% of the time, Pallas kernels for 22%

profile of v4, /device:TPU:0, one launch (start us, length us, event | category | flops | bytes accessed | tf_op | source)
XLA Modules:
  0.0 19.7 jit_solution(7036310092808541519)
XLA Ops:
  0.0 1.2 %pack.1 = (bf16[2,4,32,128]{3,2,1,0:T(8,128)(2,1)S(1)}, bf16[2,4,8,128]{3,2,1,0:T(8,128)(2,1)S(1)}, bf16[3,64,1728]{2,1,0:T(8,128)(2,1)S(1)}, f32[4,64]{1,0:T(4,...) custom-call(s32[4,32,128]{2,1,0:T(8,128)} %refs_0_.1, bf16[4,32,128]{2,1,0:T(8,128)(2,1)} %refs_1_.1, ...), custom_call_target="tpu_custom_call" | custom-call | tf_op jit(solution)/shard_map/pack/pallas_call | solution.py:58
  1.2 3.1 %collective-permute-start = (bf16[2,4,8,128]{3,2,1,0:T(8,128)(2,1)S(1)}, bf16[2,4,8,128]{3,2,1,0:T(8,128)(2,1)S(1)}, u32[]{:S(2)}, u32[]{:S(2)}) collective-permute-start(bf16[2,4,8,128]{3,2,1,0:T(8,128)(2,1)S(1)} %get-tuple-element.22), channel_id=1, source_target_pairs={{0,4},{1,0},{4,8},{5,1},{8,12},{9,5},{12,13},{13,9},{2,6},{3,2},{6... | collective-permute-start | bytes 49160 | tf_op jit(solution)/shard_map/ppermute | solution.py:494
  4.3 1.3 %prepare.1 = (bf16[3,4,1024,256]{3,2,1,0:T(8,128)(2,1)S(1)}, bf16[160,512]{1,0:T(8,128)(2,1)S(1)}, f32[8,256]{1,0:T(8,128)S(1)}, bf16[8,256]{1,0:T(8,128)(2,1)S(1)}) custom-call(bf16[3,64,1728]{2,1,0:T(8,128)(2,1)S(1)} %get-tuple-element.25.w_ref, f32[4,64]{1,0:T(4,128)S(1)} %get-tuple-element.26.embed_ref, f32[1,64]{1,0:T(1,128)S(1)} %get-tuple-element.27.gain_ref, ...), custom_call_target="tpu_custom_call" | custom-call | bytes 20000000 | tf_op jit(solution)/shard_map/prepare/pallas_call | solution.py:158
  5.7 0.1 collective-permute-done.up_ref.down_ref
  5.8 1.6 %collective-permute-start.1 = (bf16[2,2,32,128]{3,2,1,0:T(8,128)(2,1)S(1)}, bf16[2,2,32,128]{3,2,1,0:T(8,128)(2,1)S(1)}, u32[]{:S(2)}, u32[]{:S(2)}) collective-permute-start(bf16[2,2,32,128]{3,2,1,0:T(8,128)(2,1)S(1)} %get-tuple-element.23), channel_id=1, source_target_pairs={{0,2},{2,0},{1,3},{3,1},{4,6},{6,4},{5,7},{7,5},{8,10},{10,8},{9,1... | collective-permute-start | bytes 98312 | tf_op jit(solution)/shard_map/ppermute | solution.py:501
  7.3 3.0 %first.1 = (bf16[16,6,16,256]{3,2,1,0:T(8,128)(2,1)S(1)}, bf16[16,6,16,256]{3,2,1,0:T(8,128)(2,1)S(1)}, f32[2,640,256]{2,1,0:T(8,128)S(1)}) custom-call(bf16[2,4,32,128]{3,2,1,0:T(8,128)(2,1)S(1)} %get-tuple-element.24.own_ref, bf16[3,4,1024,256]{3,2,1,0:T(8,128)(2,1)S(1)} %get-tuple-element.30.w_ref, bf16[160,512]{1,0:T(8,128)(2,1)S(1)} %get-tuple-element.31.wc_ref, ...), custom_call_target="tpu_custom_call" | custom-call | flops 2500000000 | bytes 20000000 | tf_op jit(solution)/shard_map/first/pallas_call | solution.py:442
  10.3 0.0 collective-permute-done.1.next_ref
  10.3 7.5 %second.1 = f32[4,16,128]{2,1,0:T(8,128)S(1)} custom-call(bf16[2,2,32,128]{3,2,1,0:T(8,128)(2,1)S(1)} %collective-permute-done.1.next_ref, bf16[16,6,16,256]{3,2,1,0:T(8,128)(2,1)S(1)} %get-tuple-element.33.e0_ref, bf16[16,6,16,256]{3,2,1,0:T(8,128)(2,1)S(1)} %get-tuple-element.34.o0_ref, f32[2,640,256]{2,1,0:T(8,128)S(1)} %get-tuple-element.35.start_ref, ...), custom_call_target="tpu_custom_call" | custom-call | tf_op jit(solution)/shard_map/second/pallas_call | solution.py:462
  17.8 0.1 collective-permute-start.2
  17.9 1.2 %collective-permute-done.2 = f32[4,16,128]{2,1,0:T(8,128)S(1)} collective-permute-done((f32[4,16,128]{2,1,0:T(8,128)S(1)}, f32[4,16,128]{2,1,0:T(8,128)S(1)}, u32[]{:S(2)}, u32[]{:S(2)}) %collective-permute-start.2) | collective-permute-done | bytes 32800 | tf_op jit(solution)/shard_map/ppermute | solution.py:507
  19.1 0.6 %pad_maximum_fusion = f32[4,32,128]{2,1,0:T(8,128)} fusion(f32[4,16,128]{2,1,0:T(8,128)S(1)} %get-tuple-element.38, f32[4,16,128]{2,1,0:T(8,128)S(1)} %get-tuple-element.37), kind=kLoop, calls=%fused_computation | loop fusion | flops 16384 | bytes 131072 | tf_op jit(solution)/shard_map/concatenate | solution.py:510
  (2 shorter events, 0.0 us)
Async XLA Ops:
  1.2 4.5 %collective-permute-start = (bf16[2,4,8,128]{3,2,1,0:T(8,128)(2,1)S(1)}, bf16[2,4,8,128]{3,2,1,0:T(8,128)(2,1)S(1)}, u32[]{:S(2)}, u32[]{:S(2)}) collective-permute-start(bf16[2,4,8,128]{3,2,1,0:T(8,128)(2,1)S(1)} %get-tuple-element.22), channel_id=1, source_target_pairs={{0,4},{1,0},{4,8},{5,1},{8,12},{9,5},{12,13},{13,9},{2,6},{3,2},{6... | collective-permute-start | bytes 49160 | tf_op jit(solution)/shard_map/ppermute | solution.py:494
  5.8 4.5 %collective-permute-start.1 = (bf16[2,2,32,128]{3,2,1,0:T(8,128)(2,1)S(1)}, bf16[2,2,32,128]{3,2,1,0:T(8,128)(2,1)S(1)}, u32[]{:S(2)}, u32[]{:S(2)}) collective-permute-start(bf16[2,2,32,128]{3,2,1,0:T(8,128)(2,1)S(1)} %get-tuple-element.23), channel_id=1, source_target_pairs={{0,2},{2,0},{1,3},{3,1},{4,6},{6,4},{5,7},{7,5},{8,10},{10,8},{9,1... | collective-permute-start | bytes 98312 | tf_op jit(solution)/shard_map/ppermute | solution.py:501
  17.8 1.3 %collective-permute-start.2 = (f32[4,16,128]{2,1,0:T(8,128)S(1)}, f32[4,16,128]{2,1,0:T(8,128)S(1)}, u32[]{:S(2)}, u32[]{:S(2)}) collective-permute-start(f32[4,16,128]{2,1,0:T(8,128)S(1)} %second.1), channel_id=1, source_target_pairs={{0,1},{1,0},{2,3},{3,2},{4,5},{5,4},{6,7},{7,6},{8,9},{9,8},{10,11... | collective-permute-start | bytes 98312 | tf_op jit(solution)/shard_map/ppermute | solution.py:507

commit v5 on v4

--- a/solution.py
+++ b/solution.py
@@ -271,14 +271,22 @@
             for k in range(2):
                 open_ref[k, pl.ds(q * self.block, 2 * self.block), :] = value[:, k * self.lanes : (k + 1) * self.lanes]
 
-    def keep(self, ref, pair, value):
+    def keep(self, ref, pair, value, blend=None):
         half, block, mid = self.half, self.block, self.mid
         slot = pair + EDGE
-        ref[slot, pl.ds(1, half)] = value.reshape(half, SUB, self.lanes).astype(BF)
+
+        def put(slab, lane, part):
+            part = part.astype(BF)
+            if blend is not None:
+                other, mine, theirs = blend
+                part = part * mine[..., lane] + other[slot, slab, :, lane] * theirs[..., lane]
+            ref[slot, slab, :, lane] = part
+
+        put(slice(1, half + 1), slice(0, self.lanes), value.reshape(half, SUB, self.lanes))
         last = pltpu.roll(value[block - SUB :, mid:], 1, 0)
-        ref[slot, 0, :, mid:] = jnp.where(self.sub_row == 0, 0.0, last).astype(BF)
+        put(slice(0, 1), slice(mid, 2 * mid), jnp.where(self.sub_row == 0, 0.0, last)[None])
         head = pltpu.roll(value[:SUB, :mid], SUB - 1, 0)
-        ref[slot, half + 1, :, :mid] = jnp.where(self.sub_row == SUB - 1, 0.0, head).astype(BF)
+        put(slice(half + 1, half + 2), slice(0, mid), jnp.where(self.sub_row == SUB - 1, 0.0, head)[None])
 
     def reach(self, extent):
         return EDGE - (extent + 1) // 2, self.pairs + extent, extent % 2
@@ -308,7 +316,7 @@
             view(slice(2, half + 2), slice(0, mid)),
         ]
 
-    def layer(self, index, sources, e_ref, o_ref, m_ref, w_ref, b_ref, extent, open_ref=None):
+    def layer(self, index, sources, e_ref, o_ref, m_ref, w_ref, b_ref, extent, open_ref=None, blend=(None, None)):
         bias = b_ref[pl.ds(index, 1), :]
         low, n_all, shift = self.reach(extent)
         count = -(-n_all // CHUNK)
@@ -343,7 +351,7 @@
                     if y < 0 or y >= self.strip:
                         spot = self.first_row + y
                         row = row * jnp.where((spot >= 0) & (spot < self.all_rows), 1.0, 0.0).astype(F32)
-                    self.keep(o_ref if y % 2 else e_ref, y // 2, row)
+                    self.keep(o_ref if y % 2 else e_ref, y // 2, row, blend[y % 2])
 
     def logits(self, e_ref, o_ref, rw_ref, t_ref, out_ref, at):
         pairs, block, cols = self.pairs, self.block, self.cols
@@ -370,14 +378,15 @@
                 out_ref[at + r, pl.ds(k, pairs, stride=2), :] = line
 
 
-def run_first_window(s, f_ref, wc_ref, e_ref, o_ref, c_ref, m_ref, open_ref, w_ref, b_ref):
+def run_first_window(s, f_ref, wc_ref, e_ref, o_ref, c_ref, m_ref, open_ref, w_ref, b_ref, blend=(None, None)):
     extent = 2 * s.layers - 1
     s.opening(f_ref, wc_ref, open_ref, extent)
     s.layer(0, (), e_ref, o_ref, m_ref, w_ref, b_ref, extent, open_ref)
     for layer in range(1, s.layers):
         extent -= 1
         s.transform(e_ref, o_ref, c_ref, extent)
-        s.layer(layer, ((c_ref, 0),), e_ref, o_ref, m_ref, w_ref, b_ref, extent)
+        last = blend if layer == s.layers - 1 else (None, None)
+        s.layer(layer, ((c_ref, 0),), e_ref, o_ref, m_ref, w_ref, b_ref, extent, None, last)
 
 
 def first_kernel(cfg, own_ref, w_ref, wc_ref, b_ref, e0_ref, o0_ref, start_ref, c_ref, f_ref, m_ref, open_ref):
@@ -393,25 +402,25 @@
 ):
     s = Strip(cfg, b_ref.shape[1])
     s.features([next_ref[kind, r] for r in range(2) for kind in range(2)], f_ref)
-    run_first_window(s, f_ref.at[0], wc_ref, e_ref, o_ref, c_ref, m_ref, open_ref, w_ref, b_ref)
-    s.logits(e0_ref, o0_ref, rw_ref, t_ref, out_ref, 0)
     lane_id = lax.broadcasted_iota(jnp.int32, (SUB, s.lanes), 1)
     is_next = remainder(lane_id, s.mid) < s.mid // 2
-    own_part = jnp.where(is_next, 0.0, 1.0).astype(BF)[None]
-    next_part = jnp.where(is_next & s.has_next, 1.0, 0.0).astype(BF)[None]
-    reach = (s.layers + 1) // 2
-    for source, ref in ((e0_ref, e_ref), (o0_ref, o_ref)):
-        for slot in range(EDGE - reach, EDGE + s.pairs + reach):
-            ref[slot] = ref[slot] * next_part + source[slot] * own_part
+    theirs = jnp.where(is_next, 0.0, 1.0).astype(BF)[None]
+    mine = jnp.where(is_next & s.has_next, 1.0, 0.0).astype(BF)[None]
+    run_first_window(
+        s, f_ref.at[0], wc_ref, e_ref, o_ref, c_ref, m_ref, open_ref, w_ref, b_ref,
+        ((e0_ref, mine, theirs), (o0_ref, mine, theirs)),
+    )
+    s.logits(e0_ref, o0_ref, rw_ref, t_ref, out_ref, 0)
     final = (eb_ref, ob_ref)
     for layer in range(s.layers):
         extent = s.layers - 1 - layer
-        s.transform(e_ref, o_ref, side_ref, extent)
-        if layer == 0:
-            sources = ((side_ref, 2 * s.lanes),)
-        else:
+        shift = extent % 2
+        if s.layers - 1 - extent < 2:
+            s.transform(e_ref, o_ref, side_ref.at[shift], extent)
+        sources = ((side_ref.at[shift], 2 * s.lanes),)
+        if layer > 0:
             s.transform(*final, c_ref, extent)
-            sources = ((c_ref, 0), (side_ref, 2 * s.lanes))
+            sources = ((c_ref, 0),) + sources
         s.layer(layer, sources, *final, m_ref, w_ref, b_ref, extent, None if layer else start_ref)
     s.logits(*final, rw_ref, t_ref, out_ref, 2)
 
@@ -465,7 +474,7 @@
         in_specs=[vmem] * 8,
         out_specs=vmem,
         scratch_shapes=[pltpu.VMEM(buffer, BF)] * 4
-        + [pltpu.VMEM((4,) + buffer, BF)] * 2
+        + [pltpu.VMEM((4,) + buffer, BF), pltpu.VMEM((2, 4) + buffer, BF)]
         + [*scratch(cfg, lanes, 1), pltpu.VMEM((2, cfg[2] // 2 * 8, cfg[3]), F32)],
         compiler_params=pltpu.CompilerParams(vmem_limit_bytes=40 << 20),
         name="second",

time: 19.9 us -> 19.6 us (0.985)
  Pallas kernels: 13.1 us -> 12.7 us
    pallas_call x1, Pallas kernels: 7.49 us -> 7.19 us  [second_half(): pl.pallas_call(functools.partial(second_kernel, cfg), out_shape=jax.Shape...]
where the time goes in v5:
time: 19.6 us; the launch traced here: 19.4 us
  Pallas kernels  12.7 us (65%)
  starting transfers between devices  4.69 us (24%)
  waiting for transfers between devices  1.26 us (6%)
  other arithmetic  0.64 us (3%)
    pallas_call x1, Pallas kernels, second_half(): pl.pallas_call(functools.partial(second_kernel, cfg), out_shape=jax.Shape...  7.19 us
    ppermute x1, starting transfers between devices, per_device(): up = down = lax.ppermute(edge, ('space', 'chan'), chain)  3.07 us
    pallas_call x1, Pallas kernels, first_half(): pl.pallas_call(functools.partial(first_kernel, cfg), out_shape=(jax.Shape...  2.96 us
    ppermute x1, starting transfers between devices, per_device(): lax.ppermute(send, 'tm', [(t, (t - 1) % n_tm) for t in range(n_tm)])  1.56 us
    pallas_call x1, Pallas kernels, prepare(): pl.pallas_call(functools.partial(prep_kernel, layers, ch), out_shape=(jax...  1.35 us
    pallas_call x1, Pallas kernels, pack(): pl.pallas_call(functools.partial(pack_kernel, n_chan), out_shape=outs, in...  1.22 us
    ppermute x1, waiting for transfers between devices, per_device(): lax.ppermute(mine, 'chan', [(c, (c - step) % n_chan) for c in range(n_cha...  1.17 us
    concatenate x1, other arithmetic, per_device(): return jnp.concatenate(ordered, 1)  0.64 us
  transfers between devices with their start and end apart: 3, of which 2 were waited for; matrix products, arithmetic and copies ran while one was open for 0% of the time, Pallas kernels for 22%

profile of v5, /device:TPU:0, one launch (start us, length us, event | category | flops | bytes accessed | tf_op | source)
XLA Modules:
  0.0 19.4 jit_solution(11192045237017241183)
XLA Ops:
  0.0 1.2 %pack.1 = (bf16[2,4,32,128]{3,2,1,0:T(8,128)(2,1)S(1)}, bf16[2,4,8,128]{3,2,1,0:T(8,128)(2,1)S(1)}, bf16[3,64,1728]{2,1,0:T(8,128)(2,1)S(1)}, f32[4,64]{1,0:T(4,...) custom-call(s32[4,32,128]{2,1,0:T(8,128)} %refs_0_.1, bf16[4,32,128]{2,1,0:T(8,128)(2,1)} %refs_1_.1, ...), custom_call_target="tpu_custom_call" | custom-call | tf_op jit(solution)/shard_map/pack/pallas_call | solution.py:58
  1.2 3.1 %collective-permute-start = (bf16[2,4,8,128]{3,2,1,0:T(8,128)(2,1)S(1)}, bf16[2,4,8,128]{3,2,1,0:T(8,128)(2,1)S(1)}, u32[]{:S(2)}, u32[]{:S(2)}) collective-permute-start(bf16[2,4,8,128]{3,2,1,0:T(8,128)(2,1)S(1)} %get-tuple-element.22), channel_id=1, source_target_pairs={{0,4},{1,0},{4,8},{5,1},{8,12},{9,5},{12,13},{13,9},{2,6},{3,2},{6... | collective-permute-start | bytes 49160 | tf_op jit(solution)/shard_map/ppermute | solution.py:503
  4.3 1.3 %prepare.1 = (bf16[3,4,1024,256]{3,2,1,0:T(8,128)(2,1)S(1)}, bf16[160,512]{1,0:T(8,128)(2,1)S(1)}, f32[8,256]{1,0:T(8,128)S(1)}, bf16[8,256]{1,0:T(8,128)(2,1)S(1)}) custom-call(bf16[3,64,1728]{2,1,0:T(8,128)(2,1)S(1)} %get-tuple-element.25.w_ref, f32[4,64]{1,0:T(4,128)S(1)} %get-tuple-element.26.embed_ref, f32[1,64]{1,0:T(1,128)S(1)} %get-tuple-element.27.gain_ref, ...), custom_call_target="tpu_custom_call" | custom-call | bytes 20000000 | tf_op jit(solution)/shard_map/prepare/pallas_call | solution.py:158
  5.7 0.1 collective-permute-done.up_ref.down_ref
  5.8 1.6 %collective-permute-start.1 = (bf16[2,2,32,128]{3,2,1,0:T(8,128)(2,1)S(1)}, bf16[2,2,32,128]{3,2,1,0:T(8,128)(2,1)S(1)}, u32[]{:S(2)}, u32[]{:S(2)}) collective-permute-start(bf16[2,2,32,128]{3,2,1,0:T(8,128)(2,1)S(1)} %get-tuple-element.23), channel_id=1, source_target_pairs={{0,2},{2,0},{1,3},{3,1},{4,6},{6,4},{5,7},{7,5},{8,10},{10,8},{9,1... | collective-permute-start | bytes 98312 | tf_op jit(solution)/shard_map/ppermute | solution.py:510
  7.3 3.0 %first.1 = (bf16[16,6,16,256]{3,2,1,0:T(8,128)(2,1)S(1)}, bf16[16,6,16,256]{3,2,1,0:T(8,128)(2,1)S(1)}, f32[2,640,256]{2,1,0:T(8,128)S(1)}) custom-call(bf16[2,4,32,128]{3,2,1,0:T(8,128)(2,1)S(1)} %get-tuple-element.24.own_ref, bf16[3,4,1024,256]{3,2,1,0:T(8,128)(2,1)S(1)} %get-tuple-element.30.w_ref, bf16[160,512]{1,0:T(8,128)(2,1)S(1)} %get-tuple-element.31.wc_ref, ...), custom_call_target="tpu_custom_call" | custom-call | flops 2500000000 | bytes 20000000 | tf_op jit(solution)/shard_map/first/pallas_call | solution.py:451
  10.3 0.0 collective-permute-done.1.next_ref
  10.3 7.2 %second.1 = f32[4,16,128]{2,1,0:T(8,128)S(1)} custom-call(bf16[2,2,32,128]{3,2,1,0:T(8,128)(2,1)S(1)} %collective-permute-done.1.next_ref, bf16[16,6,16,256]{3,2,1,0:T(8,128)(2,1)S(1)} %get-tuple-element.33.e0_ref, bf16[16,6,16,256]{3,2,1,0:T(8,128)(2,1)S(1)} %get-tuple-element.34.o0_ref, f32[2,640,256]{2,1,0:T(8,128)S(1)} %get-tuple-element.35.start_ref, ...), custom_call_target="tpu_custom_call" | custom-call | tf_op jit(solution)/shard_map/second/pallas_call | solution.py:471
  17.5 0.1 collective-permute-start.2
  17.6 1.2 %collective-permute-done.2 = f32[4,16,128]{2,1,0:T(8,128)S(1)} collective-permute-done((f32[4,16,128]{2,1,0:T(8,128)S(1)}, f32[4,16,128]{2,1,0:T(8,128)S(1)}, u32[]{:S(2)}, u32[]{:S(2)}) %collective-permute-start.2) | collective-permute-done | bytes 32800 | tf_op jit(solution)/shard_map/ppermute | solution.py:516
  18.8 0.6 %pad_maximum_fusion = f32[4,32,128]{2,1,0:T(8,128)} fusion(f32[4,16,128]{2,1,0:T(8,128)S(1)} %get-tuple-element.38, f32[4,16,128]{2,1,0:T(8,128)S(1)} %get-tuple-element.37), kind=kLoop, calls=%fused_computation | loop fusion | flops 16384 | bytes 131072 | tf_op jit(solution)/shard_map/concatenate | solution.py:519
  (2 shorter events, 0.0 us)
Async XLA Ops:
  1.2 4.5 %collective-permute-start = (bf16[2,4,8,128]{3,2,1,0:T(8,128)(2,1)S(1)}, bf16[2,4,8,128]{3,2,1,0:T(8,128)(2,1)S(1)}, u32[]{:S(2)}, u32[]{:S(2)}) collective-permute-start(bf16[2,4,8,128]{3,2,1,0:T(8,128)(2,1)S(1)} %get-tuple-element.22), channel_id=1, source_target_pairs={{0,4},{1,0},{4,8},{5,1},{8,12},{9,5},{12,13},{13,9},{2,6},{3,2},{6... | collective-permute-start | bytes 49160 | tf_op jit(solution)/shard_map/ppermute | solution.py:503
  5.8 4.5 %collective-permute-start.1 = (bf16[2,2,32,128]{3,2,1,0:T(8,128)(2,1)S(1)}, bf16[2,2,32,128]{3,2,1,0:T(8,128)(2,1)S(1)}, u32[]{:S(2)}, u32[]{:S(2)}) collective-permute-start(bf16[2,2,32,128]{3,2,1,0:T(8,128)(2,1)S(1)} %get-tuple-element.23), channel_id=1, source_target_pairs={{0,2},{2,0},{1,3},{3,1},{4,6},{6,4},{5,7},{7,5},{8,10},{10,8},{9,1... | collective-permute-start | bytes 98312 | tf_op jit(solution)/shard_map/ppermute | solution.py:510
  17.5 1.3 %collective-permute-start.2 = (f32[4,16,128]{2,1,0:T(8,128)S(1)}, f32[4,16,128]{2,1,0:T(8,128)S(1)}, u32[]{:S(2)}, u32[]{:S(2)}) collective-permute-start(f32[4,16,128]{2,1,0:T(8,128)S(1)} %second.1), channel_id=1, source_target_pairs={{0,1},{1,0},{2,3},{3,2},{4,5},{5,4},{6,7},{7,6},{8,9},{9,8},{10,11... | collective-permute-start | bytes 98312 | tf_op jit(solution)/shard_map/ppermute | solution.py:516

commit v6 on v5

--- a/solution.py
+++ b/solution.py
@@ -139,11 +139,21 @@
                     a = dx + b
                     if layer > 0:
                         wout_ref[layer, i, pl.ds(a * 2 * ch, 2 * ch), pl.ds(b * 2 * ch, 2 * ch)] = own
-                    wout_ref[layer, i, pl.ds(lanes * 2 + a * 2 * ch, 2 * ch), pl.ds(b * 2 * ch, 2 * ch)] = side
+                    if layer > 1:
+                        wout_ref[layer, i, pl.ds(lanes * 2 + a * 2 * ch, 2 * ch), pl.ds(b * 2 * ch, 2 * ch)] = side
+                        continue
+                    spot = (2, 0, 1, 3)[a] * ch
+                    for k in range(2):
+                        lane = b * 2 * ch + (layer ^ k) * ch
+                        wout_ref[0, i, pl.ds(k * lanes + spot, ch), pl.ds(lane, ch)] = sets[2 * k][i].astype(BF)
         for i in range(4):
-            for base in (0, lanes * 2)[layer == 0 :]:
+            for base in ((), (0,), (0, lanes * 2))[layer]:
                 wout_ref[layer, i, pl.ds(base + 6 * ch, 2 * ch), pl.ds(0, 2 * ch)] = zero_block
                 wout_ref[layer, i, pl.ds(base, 2 * ch), pl.ds(2 * ch, 2 * ch)] = zero_block
+            if layer == 0:
+                for base in (0, lanes):
+                    wout_ref[0, i, pl.ds(base + 3 * ch, ch), pl.ds(0, 2 * ch)] = zero_block[:ch]
+                    wout_ref[0, i, pl.ds(base + 2 * ch, ch), pl.ds(2 * ch, 2 * ch)] = zero_block[:ch]
         bout_ref[pl.ds(layer, 1), :] = jnp.concatenate([bias_ref[pl.ds(layer, 1), :]] * 4, 1)
     read = jnp.concatenate([read_ref[...]] * 4, 1)
     high = read.astype(BF).astype(F32)
@@ -316,7 +326,7 @@
             view(slice(2, half + 2), slice(0, mid)),
         ]
 
-    def layer(self, index, sources, e_ref, o_ref, m_ref, w_ref, b_ref, extent, open_ref=None, blend=(None, None)):
+    def layer(self, index, sources, e_ref, o_ref, m_ref, w_ref, b_ref, extent, adds=(), blend=(None, None)):
         bias = b_ref[pl.ds(index, 1), :]
         low, n_all, shift = self.reach(extent)
         count = -(-n_all // CHUNK)
@@ -326,22 +336,26 @@
             spare %= 2
             size = n * self.block
             upper = lower = bias
-            if open_ref is not None:
-                at = pl.ds(begin * self.block, size)
-                upper, lower = open_ref[0, at, :] + bias, open_ref[1, at, :] + bias
+            at = pl.ds(begin * self.block, size)
+            for add in adds:
+                upper, lower = upper + add[0, at, :], lower + add[1, at, :]
             if sources:
                 first = sources[0][1]
                 depth = self.lanes * 2 * len(sources)
-                for i in range(4):
+
+                def product(i):
                     lhs = sum([self.taps(c_ref, i, low + begin, n) for c_ref, _ in sources], [])
-                    m_ref[spare, i, pl.ds(0, size)] = jnp.dot(
+                    return jnp.dot(
                         jnp.concatenate(lhs, 1),
                         w_ref[index, i, pl.ds(first, depth), :],
                         preferred_element_type=F32,
                     )
-                m = [m_ref[spare, i, pl.ds(0, size)] for i in range(4)]
-                upper = upper + m[1] + (m[0] + m[2])
-                lower = lower + m[1] - (m[2] + m[3])
+
+                for i in (1, 2):
+                    m_ref[spare, i, pl.ds(0, size)] = product(i)
+                one, two = (m_ref[spare, i, pl.ds(0, size)] for i in (1, 2))
+                upper = upper + one + two + product(0)
+                lower = lower + one - two - product(3)
             upper, lower = jnp.maximum(upper, 0.0), jnp.maximum(lower, 0.0)
             for q in range(n):
                 p = low - EDGE + begin + q
@@ -352,6 +366,39 @@
                         spot = self.first_row + y
                         row = row * jnp.where((spot >= 0) & (spot < self.all_rows), 1.0, 0.0).astype(F32)
                     self.keep(o_ref if y % 2 else e_ref, y // 2, row, blend[y % 2])
+
+    def shared_sides(self, side_ref, m_ref, w_ref, add_ref, extent):
+        half, mid, ch = self.half, self.mid, self.mid // 2
+        low, n, _ = self.reach(extent)
+        rows = n * self.block
+        sums = []
+        for k in range(2):
+            at = (1 - k) * ch
+
+            def product(i):
+                view = lambda slab, lane: side_ref[i, pl.ds(low, n), slab, :, lane].reshape(rows, mid)
+                pieces = (
+                    view(slice(1, half + 1), slice(0, mid)),
+                    view(slice(1, half + 1), slice(mid, 2 * mid)),
+                    view(slice(0, half), slice(mid, 2 * mid)),
+                    view(slice(2, half + 2), slice(0, mid)),
+                )
+                return jnp.dot(
+                    jnp.concatenate([piece[:, at : at + ch] for piece in pieces], 1),
+                    w_ref[0, i, pl.ds(k * self.lanes, self.lanes), :],
+                    preferred_element_type=F32,
+                )
+
+            for i in (1, 2):
+                m_ref[k, i, pl.ds(0, rows)] = product(i)
+            one, two = (m_ref[k, i, pl.ds(0, rows)] for i in (1, 2))
+            sums.append((one + two + product(0), one - two - product(3)))
+        first = remainder(lax.broadcasted_iota(jnp.int32, (1, self.lanes), 1), mid) < ch
+        for row, (left, right) in enumerate(zip(*sums)):
+            add_ref[0, row, pl.ds(0, rows)] = jnp.where(first, left, right)
+            crossed = jnp.where(first, right, left)
+            for lane in (0, mid):
+                add_ref[1, row, pl.ds(0, rows), lane : lane + mid] = pltpu.roll(crossed[:, lane : lane + mid], ch, 1)
 
     def logits(self, e_ref, o_ref, rw_ref, t_ref, out_ref, at):
         pairs, block, cols = self.pairs, self.block, self.cols
@@ -381,12 +428,12 @@
 def run_first_window(s, f_ref, wc_ref, e_ref, o_ref, c_ref, m_ref, open_ref, w_ref, b_ref, blend=(None, None)):
     extent = 2 * s.layers - 1
     s.opening(f_ref, wc_ref, open_ref, extent)
-    s.layer(0, (), e_ref, o_ref, m_ref, w_ref, b_ref, extent, open_ref)
+    s.layer(0, (), e_ref, o_ref, m_ref, w_ref, b_ref, extent, (open_ref,))
     for layer in range(1, s.layers):
         extent -= 1
         s.transform(e_ref, o_ref, c_ref, extent)
         last = blend if layer == s.layers - 1 else (None, None)
-        s.layer(layer, ((c_ref, 0),), e_ref, o_ref, m_ref, w_ref, b_ref, extent, None, last)
+        s.layer(layer, ((c_ref, 0),), e_ref, o_ref, m_ref, w_ref, b_ref, extent, (), last)
 
 
 def first_kernel(cfg, own_ref, w_ref, wc_ref, b_ref, e0_ref, o0_ref, start_ref, c_ref, f_ref, m_ref, open_ref):
@@ -398,7 +445,7 @@
 
 def second_kernel(
     cfg, next_ref, e0_ref, o0_ref, start_ref, w_ref, wc_ref, b_ref, rw_ref, out_ref,
-    e_ref, o_ref, eb_ref, ob_ref, c_ref, side_ref, f_ref, m_ref, open_ref, t_ref,
+    e_ref, o_ref, eb_ref, ob_ref, c_ref, side_ref, f_ref, m_ref, open_ref, t_ref, add_ref,
 ):
     s = Strip(cfg, b_ref.shape[1])
     s.features([next_ref[kind, r] for r in range(2) for kind in range(2)], f_ref)
@@ -412,16 +459,17 @@
     )
     s.logits(e0_ref, o0_ref, rw_ref, t_ref, out_ref, 0)
     final = (eb_ref, ob_ref)
-    for layer in range(s.layers):
-        extent = s.layers - 1 - layer
-        shift = extent % 2
-        if s.layers - 1 - extent < 2:
-            s.transform(e_ref, o_ref, side_ref.at[shift], extent)
-        sources = ((side_ref.at[shift], 2 * s.lanes),)
-        if layer > 0:
-            s.transform(*final, c_ref, extent)
-            sources = ((c_ref, 0),) + sources
-        s.layer(layer, sources, *final, m_ref, w_ref, b_ref, extent, None if layer else start_ref)
+    wide = s.layers // 2 * 2
+    blank = jnp.zeros(eb_ref.shape[1:], BF)
+    ob_ref[EDGE - wide // 2 - 1] = blank
+    eb_ref[EDGE + s.pairs + wide // 2] = blank
+    s.transform(e_ref, o_ref, side_ref, wide)
+    s.shared_sides(side_ref, m_ref, w_ref, add_ref, wide)
+    s.layer(0, (), *final, m_ref, w_ref, b_ref, wide, (start_ref, add_ref.at[0]))
+    s.transform(*final, c_ref, wide)
+    s.layer(1, ((c_ref, 0),), *final, m_ref, w_ref, b_ref, wide, (add_ref.at[1],))
+    s.transform(*final, c_ref, 0)
+    s.layer(2, ((c_ref, 0), (side_ref, 2 * s.lanes)), *final, m_ref, w_ref, b_ref, 0)
     s.logits(*final, rw_ref, t_ref, out_ref, 2)
 
 
@@ -439,7 +487,7 @@
     block = cfg[3] // 2
     return (
         pltpu.VMEM((windows, 4, 5, 2 * rows, cfg[3]), F32),
-        pltpu.VMEM((2, 4, CHUNK * block, lanes), F32),
+        pltpu.VMEM((2, 4, max(CHUNK, cfg[2] // 2 + cfg[0]) * block, lanes), F32),
         pltpu.VMEM(open_buffer(cfg, lanes, 2 * cfg[0] - 1), F32),
     )
 
@@ -474,8 +522,9 @@
         in_specs=[vmem] * 8,
         out_specs=vmem,
         scratch_shapes=[pltpu.VMEM(buffer, BF)] * 4
-        + [pltpu.VMEM((4,) + buffer, BF), pltpu.VMEM((2, 4) + buffer, BF)]
-        + [*scratch(cfg, lanes, 1), pltpu.VMEM((2, cfg[2] // 2 * 8, cfg[3]), F32)],
+        + [pltpu.VMEM((4,) + buffer, BF)] * 2
+        + [*scratch(cfg, lanes, 1), pltpu.VMEM((2, cfg[2] // 2 * 8, cfg[3]), F32)]
+        + [pltpu.VMEM((2,) + open_buffer(cfg, lanes, cfg[0] // 2 * 2), F32)],
         compiler_params=pltpu.CompilerParams(vmem_limit_bytes=40 << 20),
         name="second",
     )(following, *held, *weights)

time: 19.6 us -> 19.4 us (0.990)
  no operation moved by 1% of the time
where the time goes in v6:
time: 19.4 us; the launch traced here: 19.3 us
  Pallas kernels  12.6 us (65%)
  starting transfers between devices  4.69 us (24%)
  waiting for transfers between devices  1.29 us (7%)
  other arithmetic  0.64 us (3%)
    pallas_call x1, Pallas kernels, second_half(): pl.pallas_call(functools.partial(second_kernel, cfg), out_shape=jax.Shape...  7.09 us
    ppermute x1, starting transfers between devices, per_device(): up = down = lax.ppermute(edge, ('space', 'chan'), chain)  3.07 us
    pallas_call x1, Pallas kernels, first_half(): pl.pallas_call(functools.partial(first_kernel, cfg), out_shape=(jax.Shape...  2.91 us
    ppermute x1, starting transfers between devices, per_device(): lax.ppermute(send, 'tm', [(t, (t - 1) % n_tm) for t in range(n_tm)])  1.56 us
    pallas_call x1, Pallas kernels, prepare(): pl.pallas_call(functools.partial(prep_kernel, layers, ch), out_shape=(jax...  1.31 us
    pallas_call x1, Pallas kernels, pack(): pl.pallas_call(functools.partial(pack_kernel, n_chan), out_shape=outs, in...  1.22 us
    ppermute x1, waiting for transfers between devices, per_device(): lax.ppermute(mine, 'chan', [(c, (c - step) % n_chan) for c in range(n_cha...  1.17 us
    concatenate x1, other arithmetic, per_device(): return jnp.concatenate(ordered, 1)  0.64 us
  transfers between devices with their start and end apart: 3, of which 2 were waited for; matrix products, arithmetic and copies ran while one was open for 0% of the time, Pallas kernels for 22%

profile of v6, /device:TPU:0, one launch (start us, length us, event | category | flops | bytes accessed | tf_op | source)
XLA Modules:
  0.0 19.3 jit_solution(9443476577441073189)
XLA Ops:
  0.0 1.2 %pack.1 = (bf16[2,4,32,128]{3,2,1,0:T(8,128)(2,1)S(1)}, bf16[2,4,8,128]{3,2,1,0:T(8,128)(2,1)S(1)}, bf16[3,64,1728]{2,1,0:T(8,128)(2,1)S(1)}, f32[4,64]{1,0:T(4,...) custom-call(s32[4,32,128]{2,1,0:T(8,128)} %refs_0_.1, bf16[4,32,128]{2,1,0:T(8,128)(2,1)} %refs_1_.1, ...), custom_call_target="tpu_custom_call" | custom-call | tf_op jit(solution)/shard_map/pack/pallas_call | solution.py:58
  1.2 3.1 %collective-permute-start = (bf16[2,4,8,128]{3,2,1,0:T(8,128)(2,1)S(1)}, bf16[2,4,8,128]{3,2,1,0:T(8,128)(2,1)S(1)}, u32[]{:S(2)}, u32[]{:S(2)}) collective-permute-start(bf16[2,4,8,128]{3,2,1,0:T(8,128)(2,1)S(1)} %get-tuple-element.22), channel_id=1, source_target_pairs={{0,4},{1,0},{4,8},{5,1},{8,12},{9,5},{12,13},{13,9},{2,6},{3,2},{6... | collective-permute-start | bytes 49160 | tf_op jit(solution)/shard_map/ppermute | solution.py:552
  4.3 1.3 %prepare.1 = (bf16[3,4,1024,256]{3,2,1,0:T(8,128)(2,1)S(1)}, bf16[160,512]{1,0:T(8,128)(2,1)S(1)}, f32[8,256]{1,0:T(8,128)S(1)}, bf16[8,256]{1,0:T(8,128)(2,1)S(1)}) custom-call(bf16[3,64,1728]{2,1,0:T(8,128)(2,1)S(1)} %get-tuple-element.25.w_ref, f32[4,64]{1,0:T(4,128)S(1)} %get-tuple-element.26.embed_ref, f32[1,64]{1,0:T(1,128)S(1)} %get-tuple-element.27.gain_ref, ...), custom_call_target="tpu_custom_call" | custom-call | bytes 20000000 | tf_op jit(solution)/shard_map/prepare/pallas_call | solution.py:168
  5.6 0.1 collective-permute-done.up_ref.down_ref
  5.8 1.6 %collective-permute-start.1 = (bf16[2,2,32,128]{3,2,1,0:T(8,128)(2,1)S(1)}, bf16[2,2,32,128]{3,2,1,0:T(8,128)(2,1)S(1)}, u32[]{:S(2)}, u32[]{:S(2)}) collective-permute-start(bf16[2,2,32,128]{3,2,1,0:T(8,128)(2,1)S(1)} %get-tuple-element.23), channel_id=1, source_target_pairs={{0,2},{2,0},{1,3},{3,1},{4,6},{6,4},{5,7},{7,5},{8,10},{10,8},{9,1... | collective-permute-start | bytes 98312 | tf_op jit(solution)/shard_map/ppermute | solution.py:559
  7.3 2.9 %first.1 = (bf16[16,6,16,256]{3,2,1,0:T(8,128)(2,1)S(1)}, bf16[16,6,16,256]{3,2,1,0:T(8,128)(2,1)S(1)}, f32[2,640,256]{2,1,0:T(8,128)S(1)}) custom-call(bf16[2,4,32,128]{3,2,1,0:T(8,128)(2,1)S(1)} %get-tuple-element.24.own_ref, bf16[3,4,1024,256]{3,2,1,0:T(8,128)(2,1)S(1)} %get-tuple-element.30.w_ref, bf16[160,512]{1,0:T(8,128)(2,1)S(1)} %get-tuple-element.31.wc_ref, ...), custom_call_target="tpu_custom_call" | custom-call | flops 2500000000 | bytes 20000000 | tf_op jit(solution)/shard_map/first/pallas_call | solution.py:499
  10.2 0.0 collective-permute-done.1.next_ref
  10.3 7.1 %second.1 = f32[4,16,128]{2,1,0:T(8,128)S(1)} custom-call(bf16[2,2,32,128]{3,2,1,0:T(8,128)(2,1)S(1)} %collective-permute-done.1.next_ref, bf16[16,6,16,256]{3,2,1,0:T(8,128)(2,1)S(1)} %get-tuple-element.33.e0_ref, bf16[16,6,16,256]{3,2,1,0:T(8,128)(2,1)S(1)} %get-tuple-element.34.o0_ref, f32[2,640,256]{2,1,0:T(8,128)S(1)} %get-tuple-element.35.start_ref, ...), custom_call_target="tpu_custom_call" | custom-call | tf_op jit(solution)/shard_map/second/pallas_call | solution.py:519
  17.3 0.1 collective-permute-start.2
  17.4 1.2 %collective-permute-done.2 = f32[4,16,128]{2,1,0:T(8,128)S(1)} collective-permute-done((f32[4,16,128]{2,1,0:T(8,128)S(1)}, f32[4,16,128]{2,1,0:T(8,128)S(1)}, u32[]{:S(2)}, u32[]{:S(2)}) %collective-permute-start.2) | collective-permute-done | bytes 32800 | tf_op jit(solution)/shard_map/ppermute | solution.py:565
  18.6 0.6 %pad_maximum_fusion = f32[4,32,128]{2,1,0:T(8,128)} fusion(f32[4,16,128]{2,1,0:T(8,128)S(1)} %get-tuple-element.38, f32[4,16,128]{2,1,0:T(8,128)S(1)} %get-tuple-element.37), kind=kLoop, calls=%fused_computation | loop fusion | flops 16384 | bytes 131072 | tf_op jit(solution)/shard_map/concatenate | solution.py:568
  (2 shorter events, 0.0 us)
Async XLA Ops:
  1.2 4.5 %collective-permute-start = (bf16[2,4,8,128]{3,2,1,0:T(8,128)(2,1)S(1)}, bf16[2,4,8,128]{3,2,1,0:T(8,128)(2,1)S(1)}, u32[]{:S(2)}, u32[]{:S(2)}) collective-permute-start(bf16[2,4,8,128]{3,2,1,0:T(8,128)(2,1)S(1)} %get-tuple-element.22), channel_id=1, source_target_pairs={{0,4},{1,0},{4,8},{5,1},{8,12},{9,5},{12,13},{13,9},{2,6},{3,2},{6... | collective-permute-start | bytes 49160 | tf_op jit(solution)/shard_map/ppermute | solution.py:552
  5.8 4.5 %collective-permute-start.1 = (bf16[2,2,32,128]{3,2,1,0:T(8,128)(2,1)S(1)}, bf16[2,2,32,128]{3,2,1,0:T(8,128)(2,1)S(1)}, u32[]{:S(2)}, u32[]{:S(2)}) collective-permute-start(bf16[2,2,32,128]{3,2,1,0:T(8,128)(2,1)S(1)} %get-tuple-element.23), channel_id=1, source_target_pairs={{0,2},{2,0},{1,3},{3,1},{4,6},{6,4},{5,7},{7,5},{8,10},{10,8},{9,1... | collective-permute-start | bytes 98312 | tf_op jit(solution)/shard_map/ppermute | solution.py:559
  17.3 1.3 %collective-permute-start.2 = (f32[4,16,128]{2,1,0:T(8,128)S(1)}, f32[4,16,128]{2,1,0:T(8,128)S(1)}, u32[]{:S(2)}, u32[]{:S(2)}) collective-permute-start(f32[4,16,128]{2,1,0:T(8,128)S(1)} %second.1), channel_id=1, source_target_pairs={{0,1},{1,0},{2,3},{3,2},{4,5},{5,4},{6,7},{7,6},{8,9},{9,8},{10,11... | collective-permute-start | bytes 98312 | tf_op jit(solution)/shard_map/ppermute | solution.py:565

commit v7 on v6

--- a/solution.py
+++ b/solution.py
@@ -530,6 +530,35 @@
     )(following, *held, *weights)
 
 
+def join_kernel(n_chan, *refs):
+    parts, out_ref, sems = refs[:n_chan], refs[n_chan], refs[n_chan + 1]
+    strip = parts[0].shape[1]
+    chan = lax.axis_index("chan")
+    copies = []
+    for k, part in enumerate(parts):
+        start = lax.rem(chan + k, n_chan) * strip
+        if strip % 8 == 0:
+            start = pl.multiple_of(start, 8)
+        copies.append(pltpu.make_async_copy(part, out_ref.at[:, pl.ds(start, strip), :], sems.at[k]))
+    for copy in copies:
+        copy.start()
+    for copy in copies:
+        copy.wait()
+
+
+def join(n_chan, parts):
+    rounds, strip, cols = parts[0].shape
+    return pl.pallas_call(
+        functools.partial(join_kernel, n_chan),
+        out_shape=jax.ShapeDtypeStruct((rounds, n_chan * strip, cols), F32),
+        in_specs=[pl.BlockSpec(memory_space=pltpu.VMEM)] * n_chan,
+        out_specs=pl.BlockSpec(memory_space=pltpu.HBM),
+        scratch_shapes=[pltpu.SemaphoreType.DMA((n_chan,))],
+        compiler_params=pltpu.CompilerParams(vmem_limit_bytes=8 << 20),
+        name="join",
+    )(*parts)
+
+
 def per_device(sizes, events, soft_info, embed, soft_gain, conv_weights, conv_bias, readout_weight):
     n_space, n_tm, n_chan = sizes
     rounds, tile, cols = events.shape
@@ -563,9 +592,7 @@
     parts = [mine]
     for step in range(1, n_chan):
         parts.append(lax.ppermute(mine, "chan", [(c, (c - step) % n_chan) for c in range(n_chan)]))
-    chan = lax.axis_index("chan")
-    ordered = [lax.select_n((c - chan) % n_chan, *parts) for c in range(n_chan)]
-    return jnp.concatenate(ordered, 1)
+    return join(n_chan, parts)
 
 
 def solution(mesh):

time: 19.4 us -> 19.4 us (level)
  other arithmetic: 0.64 us -> 0 us
  Pallas kernels: 12.6 us -> 13.2 us
    pallas_call x0 -> x1, Pallas kernels: none -> 0.64 us  [join(): pl.pallas_call(functools.partial(join_kernel, n_chan), out_shape=jax.Shap...]
    concatenate x1 -> x0, other arithmetic: 0.64 us -> none  [per_device(): return jnp.concatenate(ordered, 1)]
where the time goes in v7:
time: 19.4 us; the launch traced here: 19.3 us
  Pallas kernels  13.2 us (68%)
  starting transfers between devices  4.69 us (24%)
  waiting for transfers between devices  1.32 us (7%)
    pallas_call x1, Pallas kernels, second_half(): pl.pallas_call(functools.partial(second_kernel, cfg), out_shape=jax.Shape...  7.09 us
    ppermute x1, starting transfers between devices, per_device(): up = down = lax.ppermute(edge, ('space', 'chan'), chain)  3.07 us
    pallas_call x1, Pallas kernels, first_half(): pl.pallas_call(functools.partial(first_kernel, cfg), out_shape=(jax.Shape...  2.91 us
    ppermute x1, starting transfers between devices, per_device(): lax.ppermute(send, 'tm', [(t, (t - 1) % n_tm) for t in range(n_tm)])  1.56 us
    pallas_call x1, Pallas kernels, prepare(): pl.pallas_call(functools.partial(prep_kernel, layers, ch), out_shape=(jax...  1.31 us
    pallas_call x1, Pallas kernels, pack(): pl.pallas_call(functools.partial(pack_kernel, n_chan), out_shape=outs, in...  1.22 us
    ppermute x1, waiting for transfers between devices, per_device(): lax.ppermute(mine, 'chan', [(c, (c - step) % n_chan) for c in range(n_cha...  1.19 us
    pallas_call x1, Pallas kernels, join(): pl.pallas_call(functools.partial(join_kernel, n_chan), out_shape=jax.Shap...  0.64 us
  transfers between devices with their start and end apart: 3, of which 2 were waited for; matrix products, arithmetic and copies ran while one was open for 0% of the time, Pallas kernels for 22%

profile of v7, /device:TPU:0, one launch (start us, length us, event | category | flops | bytes accessed | tf_op | source)
XLA Modules:
  0.0 19.3 jit_solution(6149022075776014156)
XLA Ops:
  0.0 1.2 %pack.1 = (bf16[2,4,32,128]{3,2,1,0:T(8,128)(2,1)S(1)}, bf16[2,4,8,128]{3,2,1,0:T(8,128)(2,1)S(1)}, bf16[3,64,1728]{2,1,0:T(8,128)(2,1)S(1)}, f32[4,64]{1,0:T(4,...) custom-call(s32[4,32,128]{2,1,0:T(8,128)} %refs_0_.1, bf16[4,32,128]{2,1,0:T(8,128)(2,1)} %refs_1_.1, ...), custom_call_target="tpu_custom_call" | custom-call | tf_op jit(solution)/shard_map/pack/pallas_call | solution.py:58
  1.2 3.1 %collective-permute-start = (bf16[2,4,8,128]{3,2,1,0:T(8,128)(2,1)S(1)}, bf16[2,4,8,128]{3,2,1,0:T(8,128)(2,1)S(1)}, u32[]{:S(2)}, u32[]{:S(2)}) collective-permute-start(bf16[2,4,8,128]{3,2,1,0:T(8,128)(2,1)S(1)} %get-tuple-element.22), channel_id=1, source_target_pairs={{0,4},{1,0},{4,8},{5,1},{8,12},{9,5},{12,13},{13,9},{2,6},{3,2},{6... | collective-permute-start | bytes 49160 | tf_op jit(solution)/shard_map/ppermute | solution.py:581
  4.3 1.3 %prepare.1 = (bf16[3,4,1024,256]{3,2,1,0:T(8,128)(2,1)S(1)}, bf16[160,512]{1,0:T(8,128)(2,1)S(1)}, f32[8,256]{1,0:T(8,128)S(1)}, bf16[8,256]{1,0:T(8,128)(2,1)S(1)}) custom-call(bf16[3,64,1728]{2,1,0:T(8,128)(2,1)S(1)} %get-tuple-element.25.w_ref, f32[4,64]{1,0:T(4,128)S(1)} %get-tuple-element.26.embed_ref, f32[1,64]{1,0:T(1,128)S(1)} %get-tuple-element.27.gain_ref, ...), custom_call_target="tpu_custom_call" | custom-call | bytes 20000000 | tf_op jit(solution)/shard_map/prepare/pallas_call | solution.py:168
  5.6 0.1 collective-permute-done.up_ref.down_ref
  5.8 1.6 %collective-permute-start.1 = (bf16[2,2,32,128]{3,2,1,0:T(8,128)(2,1)S(1)}, bf16[2,2,32,128]{3,2,1,0:T(8,128)(2,1)S(1)}, u32[]{:S(2)}, u32[]{:S(2)}) collective-permute-start(bf16[2,2,32,128]{3,2,1,0:T(8,128)(2,1)S(1)} %get-tuple-element.23), channel_id=1, source_target_pairs={{0,2},{2,0},{1,3},{3,1},{4,6},{6,4},{5,7},{7,5},{8,10},{10,8},{9,1... | collective-permute-start | bytes 98312 | tf_op jit(solution)/shard_map/ppermute | solution.py:588
  7.3 2.9 %first.1 = (bf16[16,6,16,256]{3,2,1,0:T(8,128)(2,1)S(1)}, bf16[16,6,16,256]{3,2,1,0:T(8,128)(2,1)S(1)}, f32[2,640,256]{2,1,0:T(8,128)S(1)}) custom-call(bf16[2,4,32,128]{3,2,1,0:T(8,128)(2,1)S(1)} %get-tuple-element.24.own_ref, bf16[3,4,1024,256]{3,2,1,0:T(8,128)(2,1)S(1)} %get-tuple-element.30.w_ref, bf16[160,512]{1,0:T(8,128)(2,1)S(1)} %get-tuple-element.31.wc_ref, ...), custom_call_target="tpu_custom_call" | custom-call | flops 2500000000 | bytes 20000000 | tf_op jit(solution)/shard_map/first/pallas_call | solution.py:499
  10.2 0.0 collective-permute-done.1.next_ref
  10.3 7.1 %second.1.refs_0_ = f32[4,16,128]{2,1,0:T(8,128)S(1)} custom-call(bf16[2,2,32,128]{3,2,1,0:T(8,128)(2,1)S(1)} %collective-permute-done.1.next_ref, bf16[16,6,16,256]{3,2,1,0:T(8,128)(2,1)S(1)} %get-tuple-element.33.e0_ref, bf16[16,6,16,256]{3,2,1,0:T(8,128)(2,1)S(1)} %get-tuple-element.34.o0_ref, f32[2,640,256]{2,1,0:T(8,128)S(1)} %get-tuple-element.35.start_ref, ...), custom_call_target="tpu_custom_call" | custom-call | tf_op jit(solution)/shard_map/second/pallas_call | solution.py:519
  17.3 0.1 collective-permute-start.2
  17.4 1.2 %collective-permute-done.2.refs_1_ = f32[4,16,128]{2,1,0:T(8,128)S(1)} collective-permute-done((f32[4,16,128]{2,1,0:T(8,128)S(1)}, f32[4,16,128]{2,1,0:T(8,128)S(1)}, u32[]{:S(2)}, u32[]{:S(2)}) %collective-permute-start.2) | collective-permute-done | bytes 32800 | tf_op jit(solution)/shard_map/ppermute | solution.py:594
  18.6 0.6 %join.1 = f32[4,32,128]{2,1,0:T(8,128)} custom-call(f32[4,16,128]{2,1,0:T(8,128)S(1)} %second.1.refs_0_, f32[4,16,128]{2,1,0:T(8,128)S(1)} %collective-permute-done.2.refs_1_), custom_call_target="tpu_custom_call" | custom-call | tf_op jit(solution)/shard_map/join/pallas_call | solution.py:551
  (1 shorter events, 0.0 us)
Async XLA Ops:
  1.2 4.5 %collective-permute-start = (bf16[2,4,8,128]{3,2,1,0:T(8,128)(2,1)S(1)}, bf16[2,4,8,128]{3,2,1,0:T(8,128)(2,1)S(1)}, u32[]{:S(2)}, u32[]{:S(2)}) collective-permute-start(bf16[2,4,8,128]{3,2,1,0:T(8,128)(2,1)S(1)} %get-tuple-element.22), channel_id=1, source_target_pairs={{0,4},{1,0},{4,8},{5,1},{8,12},{9,5},{12,13},{13,9},{2,6},{3,2},{6... | collective-permute-start | bytes 49160 | tf_op jit(solution)/shard_map/ppermute | solution.py:581
  5.8 4.5 %collective-permute-start.1 = (bf16[2,2,32,128]{3,2,1,0:T(8,128)(2,1)S(1)}, bf16[2,2,32,128]{3,2,1,0:T(8,128)(2,1)S(1)}, u32[]{:S(2)}, u32[]{:S(2)}) collective-permute-start(bf16[2,2,32,128]{3,2,1,0:T(8,128)(2,1)S(1)} %get-tuple-element.23), channel_id=1, source_target_pairs={{0,2},{2,0},{1,3},{3,1},{4,6},{6,4},{5,7},{7,5},{8,10},{10,8},{9,1... | collective-permute-start | bytes 98312 | tf_op jit(solution)/shard_map/ppermute | solution.py:588
  17.3 1.3 %collective-permute-start.2 = (f32[4,16,128]{2,1,0:T(8,128)S(1)}, f32[4,16,128]{2,1,0:T(8,128)S(1)}, u32[]{:S(2)}, u32[]{:S(2)}) collective-permute-start(f32[4,16,128]{2,1,0:T(8,128)S(1)} %second.1.refs_0_), channel_id=1, source_target_pairs={{0,1},{1,0},{2,3},{3,2},{4,5},{5,4},{6,7},{7,6},{8,9},{9,8},{10,11... | collective-permute-start | bytes 98312 | tf_op jit(solution)/shard_map/ppermute | solution.py:594
